TPU v7x, 32 devices: a whole 2x2x4 slice. The times are simulated.
32 devices in a mesh: row: 4 (over z), col: 8 (over y, x, core).
Axes of the slice: x: 2, y: 2, z: 4, core: 2. Of those that a mesh axis runs over, the one named last changes fastest.
Arguments:
- hessian: float32 [16384, 4, 8, 512], P('row', None, 'col'), may hold values from -1 to 16, as said below
- weights: bfloat16 [512, 16384], P('col', 'row'), may hold values from -6 to 6
- codes: int32 [512, 8192], P('col', 'row'), may hold values from 0 to 255
- tile_map: int32 [32, 64], P('col', 'row'), may hold values from 0 to 511
- codebooks: float32 [512, 2, 256], replicated, may hold values from -6 to 6
Outputs:
- adjusted_codebooks: float32 [512, 2, 256], replicated
Inputs may be any that keep to these rules, and one draw needn't show every extreme that they name: `hessian`: H is symmetric with a dominant positive diagonal.
All inputs are finite; a program needn't handle non-finite values.
Results may differ from a plain program's by a relative error of at most 0.0003.
Values sent between devices are 32-bit elements; how exact they have to be, the bound alone decides.
A program may use at most 192 MiB of HBM per device.

v0:
```python
import functools

import jax
import jax.numpy as jnp
from jax import lax
from jax.experimental import pallas as pl
from jax.experimental.pallas import tpu as pltpu
from jax.sharding import PartitionSpec as P

TILE_ROWS = 16
TILE_COLS = 256
STEPS = 2
LANES = 128
HALF = TILE_COLS // 2

learn_rate = 0.01
MESH = pl.DeviceIdType.MESH
NT = (((1,), (1,)), ((), ()))


def split_kernel(hessian_ref, high_ref, low_ref):
    rows, width = high_ref.shape
    stride = width // LANES
    for k in range(stride):
        x = hessian_ref[pl.ds(k, rows, stride=stride), :]
        high = x.astype(jnp.bfloat16)
        high_ref[:, k * LANES : (k + 1) * LANES] = high
        low_ref[:, k * LANES : (k + 1) * LANES] = (x - high.astype(jnp.float32)).astype(jnp.bfloat16)


def split_hessian(hessian):
    rows = hessian.shape[0]
    width = hessian.shape[1] * hessian.shape[2] * hessian.shape[3]
    stride = width // LANES
    block = min(rows, 256)
    part = jax.ShapeDtypeStruct((rows, width), jnp.bfloat16)
    spec = pl.BlockSpec((block, width), lambda i: (i, 0))
    return pl.pallas_call(
        split_kernel,
        grid=(rows // block,),
        in_specs=[pl.BlockSpec((block * stride, LANES), lambda i: (i, 0))],
        out_specs=[spec, spec],
        out_shape=[part, part],
        cost_estimate=pl.CostEstimate(flops=rows * width * 4, bytes_accessed=rows * width * 8, transcendentals=0),
        name="split_hessian",
    )(hessian.reshape(rows * stride, LANES))


def pick(table, index):
    return jnp.take_along_axis(table, index, axis=1, mode="promise_in_bounds")


def lookup(table, code):
    index = code & (LANES - 1)
    upper = code >= LANES
    tables = [jnp.broadcast_to(table[n : n + 1, :], code.shape) for n in range(4)]
    even = jnp.where(upper, pick(tables[2], index), pick(tables[0], index))
    odd = jnp.where(upper, pick(tables[3], index), pick(tables[1], index))
    return even, odd


def error_kernel(map_ref, codes_ref, weights_ref, books_ref, error_ref):
    tiles_down, tiles_across = map_ref.shape
    lane = lax.broadcasted_iota(jnp.int32, (TILE_ROWS, LANES), 1)
    is_odd = (lane & 1) == 1

    def tile(t, carry):
        i, j = t // tiles_across, t % tiles_across
        rows = pl.ds(pl.multiple_of(i * TILE_ROWS, TILE_ROWS), TILE_ROWS)
        codes = codes_ref[rows, pl.ds(pl.multiple_of(j * HALF, HALF), HALF)]
        even, odd = lookup(books_ref[map_ref[i, j]], codes)
        for half in range(2):
            source = (lane >> 1) + half * (LANES // 2)
            value = jnp.where(is_odd, pick(odd, source), pick(even, source))
            columns = pl.ds(pl.multiple_of(j * TILE_COLS + half * LANES, LANES), LANES)
            error_ref[rows, columns] = value - weights_ref[rows, columns].astype(jnp.float32)
        return carry

    lax.fori_loop(0, tiles_down * tiles_across, tile, 0, unroll=4)


def shift_kernel(run, gap, col_ref, map_ref, codes_ref, error_ref, new_ref, old_ref, out_ref):
    rows_here, pairs = codes_ref.shape
    down, across = rows_here // TILE_ROWS, pairs // HALF
    top = pl.program_id(0) * down
    lane = lax.broadcasted_iota(jnp.int32, (TILE_ROWS, LANES), 1)
    is_odd = (lane & 1) == 1
    begin = col_ref[0] * run

    def table(i, column):
        place = (column // run) * gap + begin + column % run
        book = map_ref[top + i, place // TILE_COLS]
        return new_ref[book] - old_ref[book]

    def tile(t, carry):
        i, j = t // across, t % across
        rows = pl.ds(pl.multiple_of(i * TILE_ROWS, TILE_ROWS), TILE_ROWS)
        codes = codes_ref[rows, pl.ds(pl.multiple_of(j * HALF, HALF), HALF)]
        even, odd = lookup(table(i, j * TILE_COLS), codes)
        if run % TILE_COLS:
            even2, odd2 = lookup(table(i, j * TILE_COLS + LANES), codes)
            second = lane >= LANES // 2
            even, odd = jnp.where(second, even2, even), jnp.where(second, odd2, odd)
        for half in range(2):
            source = (lane >> 1) + half * (LANES // 2)
            value = jnp.where(is_odd, pick(odd, source), pick(even, source))
            columns = pl.ds(pl.multiple_of(j * TILE_COLS + half * LANES, LANES), LANES)
            out_ref[rows, columns] = error_ref[rows, columns] + value
        return carry

    lax.fori_loop(0, down * across, tile, 0, unroll=4)


def shift(run, gap, full_map, codes, error, new, old):
    m, k = error.shape
    block = min(m, 128)
    col = jnp.full((1,), lax.axis_index("col"), jnp.int32)
    books = pl.BlockSpec((new.shape[0] // 4, 4, LANES), lambda i: (0, 0, 0))
    spec = pl.BlockSpec((block, k), lambda i: (i, 0))
    return pl.pallas_call(
        functools.partial(shift_kernel, run, gap),
        grid=(m // block,),
        in_specs=[SMEM, SMEM, pl.BlockSpec((block, k // 2), lambda i: (i, 0)), spec, books, books],
        out_specs=spec,
        out_shape=jax.ShapeDtypeStruct((m, k), jnp.float32),
        name="shift",
    )(col, full_map, codes, error, new.reshape(-1, 4, LANES), old.reshape(-1, 4, LANES))


VMEM = pl.BlockSpec(memory_space=pltpu.VMEM)
SMEM = pl.BlockSpec(memory_space=pltpu.SMEM)


def errors(tile_map, codes, weights, books):
    return pl.pallas_call(
        error_kernel,
        in_specs=[SMEM, VMEM, VMEM, VMEM],
        out_specs=VMEM,
        out_shape=jax.ShapeDtypeStruct(weights.shape, jnp.float32),
        name="errors",
    )(tile_map, codes, weights, books.reshape(-1, 4, LANES))


def product_kernel(chunks, error_ref, high_ref, low_ref, out_ref, error_high, error_low, made, pair_in, pair_sum, chip_in, pair_send, pair_recv, chip_send, chip_recv):
    n = pl.program_id(0)
    r, c = lax.axis_index("row"), lax.axis_index("col")
    chips = made.shape[1]
    block = made.shape[4]
    chip, core = c // 2, lax.rem(c, 2)
    others = [lax.rem(chip + d, chips) for d in range(chips)]

    @pl.when(n == 0)
    def _():
        barrier = pltpu.get_barrier_semaphore()
        pl.semaphore_signal(barrier, inc=1, device_id=(r, chip * 2 + 1 - core), device_id_type=MESH)
        for d in range(1, chips):
            pl.semaphore_signal(barrier, inc=1, device_id=(r, others[d] * 2 + core), device_id_type=MESH)
        x = error_ref[...]
        high = x.astype(jnp.bfloat16)
        error_high[...] = high
        error_low[...] = (x - high.astype(jnp.float32)).astype(jnp.bfloat16)
        pl.semaphore_wait(barrier, chips)

    def to_pair(k):
        return pltpu.make_async_remote_copy(
            src_ref=made.at[k, :, 1 - core],
            dst_ref=pair_in.at[k],
            send_sem=pair_send.at[k],
            recv_sem=pair_recv.at[k],
            device_id=(r, chip * 2 + 1 - core),
            device_id_type=MESH,
        )

    def to_chip(k, d):
        return pltpu.make_async_remote_copy(
            src_ref=pair_sum.at[k, others[d]],
            dst_ref=chip_in.at[d - 1, k],
            send_sem=chip_send.at[d - 1, k],
            recv_sem=chip_recv.at[d - 1, k],
            device_id=(r, others[d] * 2 + core),
            device_id_type=MESH,
        )

    def add_pair(k):
        to_pair(k).wait_recv()
        pair_sum[k] = made[k, :, core] + pair_in[k]
        for d in range(1, chips):
            to_chip(k, d).start()

    dot = functools.partial(lax.dot_general, dimension_numbers=NT, preferred_element_type=jnp.float32)
    total = dot(error_high[...], low_ref[...]) + dot(error_low[...], high_ref[...])
    total = total + dot(error_high[...], high_ref[...])
    made[n] = total.reshape(made.shape[1:])
    to_pair(n).start()

    @pl.when(n > 0)
    def _():
        add_pair(n - 1)

    @pl.when(n == chunks - 1)
    def _():
        add_pair(n)

        def finish(k, carry):
            total = pair_sum[k, chip]
            for d in range(1, chips):
                to_chip(k, d).wait_recv()
                total = total + chip_in[d - 1, k]
            out_ref[:, pl.ds(pl.multiple_of(k * block, block), block)] = total
            to_pair(k).wait_send()
            for d in range(1, chips):
                to_chip(k, d).wait_send()
            return carry

        lax.fori_loop(0, chunks, finish, 0)


def product(n_col, error, high, low):
    m, k = error.shape
    n = high.shape[0]
    block = min(n, 512)
    chunks = n // block
    chips = n_col // 2
    rows = m // n_col
    spec = pl.BlockSpec((block, k), lambda i: (i, 0))
    dma = pltpu.SemaphoreType.DMA
    return pl.pallas_call(
        functools.partial(product_kernel, chunks),
        grid=(chunks,),
        in_specs=[pl.BlockSpec((m, k), lambda i: (0, 0)), spec, spec],
        out_specs=pl.BlockSpec((rows, n), lambda i: (0, 0)),
        out_shape=jax.ShapeDtypeStruct((rows, n), jnp.float32),
        scratch_shapes=[
            pltpu.VMEM((m, k), jnp.bfloat16),
            pltpu.VMEM((m, k), jnp.bfloat16),
            pltpu.VMEM((chunks, chips, 2, rows, block), jnp.float32),
            pltpu.VMEM((chunks, chips, rows, block), jnp.float32),
            pltpu.VMEM((chunks, chips, rows, block), jnp.float32),
            pltpu.VMEM((chips - 1, chunks, rows, block), jnp.float32),
            dma((chunks,)),
            dma((chunks,)),
            dma((chips - 1, chunks)),
            dma((chips - 1, chunks)),
        ],
        compiler_params=pltpu.CompilerParams(collective_id=1, has_side_effects=True, vmem_limit_bytes=56 * 2**20),
        cost_estimate=pl.CostEstimate(flops=6 * m * n * k, bytes_accessed=4 * n * k + 4 * m * (n + k), transcendentals=0),
        name="product",
    )(error, high, low)


def scatter_kernel(map_ref, codes_ref, grad_ref, books_ref):
    tiles_down, tiles_across = map_ref.shape
    shape = (TILE_ROWS, LANES)
    lane = lax.broadcasted_iota(jnp.int32, shape, 1)
    first = lane < LANES // 2
    even_index = (2 * lane) & (LANES - 1)
    line = lax.broadcasted_iota(jnp.int32, (8, LANES), 0)
    is_odd = (line & 1) == 1
    is_upper = (line & 2) == 2
    is_low = lax.broadcasted_iota(jnp.int32, (8, HALF * TILE_ROWS), 0) >= 4
    entry = lax.broadcasted_iota(jnp.int32, (LANES, LANES), 0)
    books_ref[...] = jnp.zeros_like(books_ref)

    def tile(t, carry):
        i, j = t // tiles_across, t % tiles_across
        rows = pl.ds(pl.multiple_of(i * TILE_ROWS, TILE_ROWS), TILE_ROWS)
        codes = codes_ref[rows, pl.ds(pl.multiple_of(j * HALF, HALF), HALF)]
        left = grad_ref[rows, pl.ds(pl.multiple_of(j * TILE_COLS, LANES), LANES)]
        right = grad_ref[rows, pl.ds(pl.multiple_of(j * TILE_COLS + LANES, LANES), LANES)]
        even = jnp.where(first, pick(left, even_index), pick(right, even_index))
        odd = jnp.where(first, pick(left, even_index + 1), pick(right, even_index + 1))
        index = codes & (LANES - 1)
        upper = jnp.where(codes >= LANES, 1, 0)
        values, hots = [], []
        for n in range(TILE_ROWS):
            value = jnp.where(is_odd, odd[n : n + 1, :], even[n : n + 1, :])
            fits = is_upper == (jnp.broadcast_to(upper[n : n + 1, :], (8, LANES)) == 1)
            values.append(jnp.where(fits, value, 0.0))
            hots.append(jnp.where(entry == index[n : n + 1, :], 1.0, 0.0).astype(jnp.bfloat16))
        value = jnp.concatenate(values, axis=1)
        high = value.astype(jnp.bfloat16).astype(jnp.float32)
        parts = jnp.where(is_low, value - high, high).astype(jnp.bfloat16)
        sums = lax.dot_general(parts, jnp.concatenate(hots, axis=1), NT, preferred_element_type=jnp.float32)
        book = map_ref[i, j]
        books_ref[book] += sums[0:4, :] + sums[4:8, :]
        return carry

    lax.fori_loop(0, tiles_down * tiles_across, tile, 0, unroll=2)


def scatter(tile_map, codes, grad, books):
    total = pl.pallas_call(
        scatter_kernel,
        in_specs=[SMEM, VMEM, VMEM],
        out_specs=VMEM,
        out_shape=jax.ShapeDtypeStruct((books.shape[0] // 4, 4, LANES), jnp.float32),
        name="scatter",
    )(tile_map, codes, grad)
    return total.reshape(books.shape)


def update_kernel(n_row, n_col, grad_ref, books_ref, map_ref, out_ref, maps_ref, col_in, row_sum, row_in, col_send, col_recv, row_send, row_recv, row_send2, row_recv2, col_send2, col_recv2, map_send, map_recv, map_send2, map_recv2):
    r, c = lax.axis_index("row"), lax.axis_index("col")
    wide = grad_ref.shape[0] // n_col
    thin = wide // n_row
    cols = [lax.rem(c + d, n_col) for d in range(n_col)]
    rows = [lax.rem(r + d, n_row) for d in range(n_row)]

    barrier = pltpu.get_barrier_semaphore()
    for d in range(1, n_col):
        pl.semaphore_signal(barrier, inc=1, device_id=(r, cols[d]), device_id_type=MESH)
    for d in range(1, n_row):
        pl.semaphore_signal(barrier, inc=1, device_id=(rows[d], c), device_id_type=MESH)
    pl.semaphore_wait(barrier, n_col + n_row - 2)

    def piece(index, size):
        return pl.ds(pl.multiple_of(index * size, size), size)

    def send(src, dst, sends, recvs, d, device):
        copy = pltpu.make_async_remote_copy(
            src_ref=src, dst_ref=dst, send_sem=sends.at[d], recv_sem=recvs.at[d], device_id=device, device_id_type=MESH
        )
        copy.start()
        return copy

    first = [
        send(grad_ref.at[piece(cols[d], wide)], col_in.at[d], col_send, col_recv, d, (r, cols[d])) for d in range(1, n_col)
    ]
    maps = [send(map_ref, maps_ref.at[r, c], map_send, map_recv, d, (r, cols[d])) for d in range(1, n_col)]
    maps_ref[r, c] = map_ref[...]
    total = grad_ref[piece(c, wide), :]
    for d, copy in enumerate(first, 1):
        copy.wait_recv()
        total = total + col_in[d]
    row_sum[...] = total
    second = [
        send(row_sum.at[piece(rows[d], thin)], row_in.at[d], row_send, row_recv, d, (rows[d], c)) for d in range(1, n_row)
    ]
    for copy in maps:
        copy.wait_recv()
    lines = [send(maps_ref.at[r], maps_ref.at[r], map_send2, map_recv2, d, (rows[d], c)) for d in range(1, n_row)]
    total = row_sum[piece(r, thin), :]
    for d, copy in enumerate(second, 1):
        copy.wait_recv()
        total = total + row_in[d]
    mine = piece(c * n_row + r, thin)
    out_ref[mine, :] = books_ref[mine, :] - learn_rate * (2.0 * total)
    third = [send(out_ref.at[mine], out_ref.at[mine], row_send2, row_recv2, d, (rows[d], c)) for d in range(1, n_row)]
    for copy in third:
        copy.wait_recv()
    whole = piece(c, wide)
    fourth = [send(out_ref.at[whole], out_ref.at[whole], col_send2, col_recv2, d, (r, cols[d])) for d in range(1, n_col)]
    for copy in fourth:
        copy.wait_recv()
    for copy in lines:
        copy.wait_recv()
    for copy in first + second + third + fourth + maps + lines:
        copy.wait_send()


def update(n_row, n_col, grad, books, padded):
    wide = books.shape[0] // n_col
    thin = wide // n_row
    dma = pltpu.SemaphoreType.DMA
    return pl.pallas_call(
        functools.partial(update_kernel, n_row, n_col),
        in_specs=[VMEM, VMEM, VMEM],
        out_specs=[VMEM, VMEM],
        out_shape=[
            jax.ShapeDtypeStruct(books.shape, jnp.float32),
            jax.ShapeDtypeStruct((n_row, n_col) + padded.shape, jnp.int32),
        ],
        scratch_shapes=[
            pltpu.VMEM((n_col, wide, LANES), jnp.float32),
            pltpu.VMEM((wide, LANES), jnp.float32),
            pltpu.VMEM((n_row, thin, LANES), jnp.float32),
            dma((n_col,)),
            dma((n_col,)),
            dma((n_row,)),
            dma((n_row,)),
            dma((n_row,)),
            dma((n_row,)),
            dma((n_col,)),
            dma((n_col,)),
            dma((n_col,)),
            dma((n_col,)),
            dma((n_row,)),
            dma((n_row,)),
        ],
        compiler_params=pltpu.CompilerParams(collective_id=0, has_side_effects=True),
        name="update",
    )(grad, books, padded)


def per_device(n_row, n_col, hessian, weights, codes, tile_map, codebooks):
    count, parts, entries = codebooks.shape
    books = codebooks.reshape(count, parts, entries // LANES, LANES).transpose(0, 2, 1, 3).reshape(-1, LANES)
    high, low = split_hessian(hessian)
    run = hessian.shape[2] * hessian.shape[3]
    down, across = tile_map.shape
    padded = jnp.pad(tile_map, ((0, -down % 8), (0, -across % LANES)))
    error = errors(tile_map, codes, weights, books)
    piece = lax.all_to_all(error, "col", split_axis=1, concat_axis=0, tiled=True)
    piece, held_codes = lax.optimization_barrier((piece, codes))
    spread = lax.all_gather(piece, "row", axis=1, tiled=True)
    code_piece = lax.all_to_all(held_codes, "col", split_axis=1, concat_axis=0, tiled=True)
    code_spread = None
    for step in range(STEPS):
        grad = product(n_col, spread, high, low)
        if code_spread is None:
            grad, code_piece = lax.optimization_barrier((grad, code_piece))
            code_spread = lax.all_gather(code_piece, "row", axis=1, tiled=True)
        old = books
        books, maps = update(n_row, n_col, scatter(tile_map, codes, grad, books), books, padded)
        if step < STEPS - 1:
            full_map = maps[:, :, :down, :across].transpose(1, 2, 0, 3).reshape(n_col * down, n_row * across)
            spread = shift(run, n_col * run, full_map, code_spread, spread, books, old)
    return books.reshape(count, entries // LANES, parts, LANES).transpose(0, 2, 1, 3).reshape(codebooks.shape)


def solution(mesh):
    placed = (P("row", None, "col", None), P("col", "row"), P("col", "row"), P("col", "row"), P())
    body = functools.partial(per_device, mesh.shape["row"], mesh.shape["col"])
    return jax.shard_map(body, mesh=mesh, in_specs=placed, out_specs=P(), check_vma=False)
```

profile of v0, /device:TPU:0, one launch (start us, length us, event | category | flops | bytes accessed | tf_op | source)
XLA Modules:
  0.0 387.8 jit_solution(237079612428604356)
XLA Ops:
  6.5 0.0 all-gather.3.cloned.1.call-start
  6.5 6.1 %errors.1 = f32[64,4096]{1,0:T(8,128)} custom-call(s32[4,16]{1,0:T(4,128)} %map_ref.5, s32[64,2048]{1,0:T(8,128)} %codes_ref.5, bf16[64,4096]{1,0:T(8,128)(2,1)} %weights_ref.1, f32[512,4,128]{2,1,0:T(4,128)} %bitcast.34), custom_call_target="tpu_custom_call" | custom-call | tf_op jit(solution)/shard_map/errors/pallas_call | solution.py:135
  12.6 1.3 copy.15
  13.9 20.4 %all_to_all.38 = f32[64,8,512]{2,0,1:T(8,128)} all-to-all(f32[64,8,512]{2,0,1:T(8,128)S(1)} %bitcast.42), channel_id=1, replica_groups=mesh['row'=4,'col'=8] {'col'}, dimensions={1} | all-to-all | bytes 2097152 | tf_op jit(solution)/shard_map/all_to_all | solution.py:403
  34.4 0.0 all-gather.3.cloned.1.call-update
  34.4 0.0 copy-start
  34.4 33.8 %split_hessian.1 = (bf16[4096,2048]{1,0:T(8,128)(2,1)}, bf16[4096,2048]{1,0:T(8,128)(2,1)}) custom-call(f32[65536,128]{1,0:T(8,128)} %bitcast.33), custom_call_target="tpu_custom_call" | custom-call | flops 33554432 | bytes 67108864 | tf_op jit(solution)/shard_map/split_hessian/pallas_call | solution.py:38
  68.2 0.0 copy-done
  68.2 0.8 copy.16
  69.0 3.5 all-to-all-start.1
  72.5 0.0 all-gather.5.cloned.1.call-start
  72.6 42.1 %all-gather.3.cloned.1.call-done.error_ref = f32[512,2048]{1,0:T(8,128)} async-done(((f32[512,512]{1,0:T(8,128)}), f32[512,2048]{1,0:T(8,128)}) %all-gather.3.cloned.1.call-update) | async-done | bytes 4194320 | tf_op jit(solution)/shard_map/all_gather | solution.py:405
  114.7 0.0 copy-start.2
  114.7 60.2 %product.2.grad_ref = f32[64,4096]{1,0:T(8,128)} custom-call(f32[512,2048]{1,0:T(8,128)} %all-gather.3.cloned.1.call-done.error_ref, bf16[4096,2048]{1,0:T(8,128)(2,1)} %get-tuple-element.15.high_ref, bf16[4096,2048]{1,0:T(8,128)(2,1)} %get-tuple-element.16.low_ref), custom_call_target="tpu_custom_call" | custom-call | flops 25769803776 | bytes 46137344 | tf_op jit(solution)/shard_map/product/pallas_call | solution.py:227
  174.8 0.0 all-to-all-done.1
  174.9 0.0 copy-start.1
  174.9 0.8 copy-done.1
  175.6 0.0 all-gather.5.cloned.1.call-update
  175.7 0.0 copy-done.2
  175.7 0.6 pad.4.map_ref
  176.3 17.1 %scatter.2 = f32[512,4,128]{2,1,0:T(4,128)} custom-call(s32[4,16]{1,0:T(4,128)} %map_ref.5, s32[64,2048]{1,0:T(8,128)} %codes_ref.5, f32[64,4096]{1,0:T(8,128)} %product.2.grad_ref), custom_call_target="tpu_custom_call" | custom-call | tf_op jit(solution)/shard_map/scatter/pallas_call | solution.py:292
  193.4 46.7 %update.2 = (f32[2048,128]{1,0:T(8,128)}, s32[4,8,8,128]{3,2,1,0:T(8,128)}) custom-call(f32[2048,128]{1,0:T(8,128)} %bitcast.41, f32[2048,128]{1,0:T(8,128)} %bitcast.35, s32[8,128]{1,0:T(8,128)} %pad.4.map_ref), custom_call_target="tpu_custom_call" | custom-call | tf_op jit(solution)/shard_map/update/pallas_call | solution.py:365
  240.1 0.9 slice_bitcast_fusion
  241.1 0.7 reshape.37.map_ref
  241.8 0.0 all-gather.5.cloned.1.call-done.codes_ref
  241.8 18.6 %shift.1.error_ref = f32[512,2048]{1,0:T(8,128)} custom-call(s32[1]{0:T(128)} %bitcast.col_ref, s32[32,64]{1,0:T(8,128)} %reshape.37.map_ref, s32[512,1024]{1,0:T(8,128)} %all-gather.5.cloned.1.call-done.codes_ref, f32[512,2048]{1,0:T(8,128)} %all-gather.3.cloned.1.call-done.error_ref, f32[512,4,128]{2,1,0:T(4,128)} %bitcast.38, f32[512,4,128]{2,1,0:T(4,128)} %bitcast.36), custom_call_target="tpu_custom_call" | custom-call | tf_op jit(solution)/shard_map/shift/pallas_call | solution.py:120
  260.4 61.8 %product.3.grad_ref = f32[64,4096]{1,0:T(8,128)} custom-call(f32[512,2048]{1,0:T(8,128)} %shift.1.error_ref, bf16[4096,2048]{1,0:T(8,128)(2,1)} %get-tuple-element.15.high_ref, bf16[4096,2048]{1,0:T(8,128)(2,1)} %get-tuple-element.16.low_ref), custom_call_target="tpu_custom_call" | custom-call | flops 25769803776 | bytes 46137344 | tf_op jit(solution)/shard_map/product/pallas_call | solution.py:227
  322.3 17.1 %scatter.3 = f32[512,4,128]{2,1,0:T(4,128)} custom-call(s32[4,16]{1,0:T(4,128)} %map_ref.5, s32[64,2048]{1,0:T(8,128)} %codes_ref.5, f32[64,4096]{1,0:T(8,128)} %product.3.grad_ref), custom_call_target="tpu_custom_call" | custom-call | tf_op jit(solution)/shard_map/scatter/pallas_call | solution.py:292
  339.4 39.0 %update.3 = (f32[2048,128]{1,0:T(8,128)}, s32[4,8,8,128]{3,2,1,0:T(8,128)}) custom-call(f32[2048,128]{1,0:T(8,128)} %bitcast.40, f32[2048,128]{1,0:T(8,128)} %get-tuple-element.21.books_ref, s32[8,128]{1,0:T(8,128)} %pad.4.map_ref), custom_call_target="tpu_custom_call" | custom-call | tf_op jit(solution)/shard_map/update/pallas_call | solution.py:365
  378.4 2.6 copy.18
  (1 shorter events, 0.0 us)
Async XLA Ops:
  6.5 108.1 %all-gather.3.cloned.1.call-start = ((), (), s32[]{:S(2)}) async-start(), calls=%async_computation.2 | async-start | bytes 5242880 | tf_op jit(solution)/shard_map/all_gather | solution.py:405
  34.4 33.8 %copy-start = (s32[64,2048]{1,0:T(8,128)S(1)}, s32[64,2048]{1,0:T(8,128)}, u32[]{:S(2)}) copy-start(s32[64,2048]{1,0:T(8,128)} %codes_ref.5) | copy-start | bytes 1572868
  69.0 105.8 %all-to-all-start.1 = ((s32[64,8,256]{2,0,1:T(8,128)}), s32[64,8,256]{2,0,1:T(8,128)S(1)}, u32[]{:S(2)}, u32[]{:S(2)}) async-start(s32[64,8,256]{2,0,1:T(8,128)} %bitcast.32), calls=%async_computation.1 | async-start | bytes 1048576 | tf_op jit(solution)/shard_map/all_to_all | solution.py:406
  72.5 169.3 %all-gather.5.cloned.1.call-start = ((), (), s32[]{:S(2)}) async-start(), calls=%async_computation.3 | async-start | bytes 2621440 | tf_op jit(solution)/shard_map/all_gather | solution.py:412
  114.7 61.0 %copy-start.2 = (s32[4,16]{1,0:T(4,128)S(1)}, s32[4,16]{1,0:T(4,128)}, u32[]{:S(2)}) copy-start(s32[4,16]{1,0:T(4,128)} %map_ref.5) | copy-start | bytes 772
  174.9 0.8 copy-start.1
Sparse Core Ops, SparseCore 0:
  34.5 80.0 all-gather.2
  175.8 52.9 all-gather.4
where the time goes:
time: 390 us; the launch traced here: 388 us
  Pallas kernels  300 us (77%)
  waiting for transfers between devices  42.1 us (11%)
  blocking collectives  20.4 us (5%)
  between operations  13.5 us (3%)
  local copies, waits for them, and re-layouts  7.75 us (2%)
    pallas_call x2, Pallas kernels, product(): pl.pallas_call(functools.partial(product_kernel, chunks), grid=(chunks,),...  122 us
    pallas_call x2, Pallas kernels, update(): pl.pallas_call(functools.partial(update_kernel, n_row, n_col), in_specs=[...  85.7 us
    all_gather x1, waiting for transfers between devices, per_device(): spread = lax.all_gather(piece, 'row', axis=1, tiled=True)  42.1 us
    pallas_call x2, Pallas kernels, scatter(): pl.pallas_call(scatter_kernel, in_specs=[SMEM, VMEM, VMEM], out_specs=VME...  34.2 us
    pallas_call x1, Pallas kernels, split_hessian(): pl.pallas_call(split_kernel, grid=(rows // block,), in_specs=[pl.BlockSpe...  33.8 us
    all_to_all x1, blocking collectives, per_device(): lax.all_to_all(error, 'col', split_axis=1, concat_axis=0, tiled=True)  20.4 us
    pallas_call x1, Pallas kernels, shift(): pl.pallas_call(functools.partial(shift_kernel, run, gap), grid=(m // bloc...  18.6 us
  transfers between devices with their start and end apart: 3, of which 1 were waited for; matrix products, arithmetic and copies ran while one was open for 1% of the time, Pallas kernels for 41%

commit v1 on v0

v1 whole, which is shorter than its diff:
```python
import functools

import jax
import jax.numpy as jnp
from jax import lax
from jax.experimental import pallas as pl
from jax.experimental.pallas import tpu as pltpu
from jax.sharding import PartitionSpec as P

TILE_ROWS = 16
TILE_COLS = 256
STEPS = 2
LANES = 128
HALF = TILE_COLS // 2
CHUNK_TILES = 2
LOW = 32

learn_rate = 0.01
MESH = pl.DeviceIdType.MESH
NT = (((1,), (1,)), ((), ()))
VMEM = pl.BlockSpec(memory_space=pltpu.VMEM)
SMEM = pl.BlockSpec(memory_space=pltpu.SMEM)
ANY = pl.BlockSpec(memory_space=pl.ANY)
VMEM_BYTES = 62 * 2**20


def pick(table, index):
    return jnp.take_along_axis(table, index, axis=1, mode="promise_in_bounds")


def lookup(table, code):
    index = code & (LANES - 1)
    upper = code >= LANES
    tables = [jnp.broadcast_to(table[n : n + 1, :], code.shape) for n in range(4)]
    even = jnp.where(upper, pick(tables[2], index), pick(tables[0], index))
    odd = jnp.where(upper, pick(tables[3], index), pick(tables[1], index))
    return even, odd


def split_pairs(left, right):
    lane = lax.broadcasted_iota(jnp.int32, left.shape, 1)
    first = lane < LANES // 2
    index = (2 * lane) & (LANES - 1)
    even = jnp.where(first, pick(left, index), pick(right, index))
    odd = jnp.where(first, pick(left, index + 1), pick(right, index + 1))
    return even, odd


def halves(x):
    high = x.astype(jnp.bfloat16)
    return high, (x - high.astype(jnp.float32)).astype(jnp.bfloat16)


def three_products(a_high, a_low, b_high, b_low):
    dot = functools.partial(jnp.dot, preferred_element_type=jnp.float32)
    return dot(a_high, b_low) + dot(a_low, b_high) + dot(a_high, b_high)


def flip(chip, mask):
    bit = 0
    while mask >> bit:
        if (mask >> bit) & 1:
            size = 1 << bit
            chip = chip + (1 - 2 * lax.rem(chip // size, 2)) * size
        bit += 1
    return chip


def rows_of(index, size):
    return pl.ds(pl.multiple_of(index * size, size), size)


def first_kernel(n_col, chunks, map_ref, codes_ref, weights_ref, books_ref, hessian_ref, part_ref, high_out, low_out, errors, e_high, e_low, h_in, h_high, h_low, hop_send, hop_recv, pair_send, pair_recv, in_sem, high_sem, low_sem):
    r, c = lax.axis_index("row"), lax.axis_index("col")
    chip, core = c // 2, lax.rem(c, 2)
    chips = n_col // 2
    dims = chips.bit_length() - 1
    rows = codes_ref.shape[0]
    width = h_in.shape[3]
    pairs = CHUNK_TILES * HALF
    pair = (r, chip * 2 + 1 - core)

    barrier = pltpu.get_barrier_semaphore()
    for d in range(dims):
        pl.semaphore_signal(barrier, inc=1, device_id=(r, flip(chip, 1 << d) * 2 + core), device_id_type=MESH)
    pl.semaphore_signal(barrier, inc=1, device_id=pair, device_id_type=MESH)

    def fetch(k, slot):
        def one(n, carry):
            for parity in range(2):
                pltpu.make_async_copy(
                    hessian_ref.at[rows_of(k, pairs), parity, n, 0],
                    h_in.at[slot, parity, :, rows_of(n, LANES)],
                    in_sem.at[slot],
                ).start()
            return carry

        lax.fori_loop(0, width // LANES, one, 0)

    def out_copies(k, slot):
        return [
            pltpu.make_async_copy(h_high.at[slot], high_out.at[k], high_sem.at[slot]),
            pltpu.make_async_copy(h_low.at[slot], low_out.at[k], low_sem.at[slot]),
        ]

    fetch(0, 0)
    if chunks > 1:
        fetch(1, 1)

    def order(phase):
        return [(phase + i) % dims for i in range(dims)]

    def last(mask, phase):
        return max([i for i, d in enumerate(order(phase)) if (mask >> d) & 1], default=-1)

    def block(k, mask, which):
        return errors.at[k, rows_of(flip(chip, mask) * 2 + which, rows)]

    def hop(k, mask, dim):
        here = block(k, mask, core)
        target = mask | (1 << dim)
        return pltpu.make_async_remote_copy(
            src_ref=here,
            dst_ref=here,
            send_sem=hop_send.at[k, target],
            recv_sem=hop_recv.at[k, target],
            device_id=(r, flip(chip, 1 << dim) * 2 + core),
            device_id_type=MESH,
        )

    def across(k, mask):
        here = block(k, mask, core)
        return pltpu.make_async_remote_copy(
            src_ref=here,
            dst_ref=here,
            send_sem=pair_send.at[k, mask],
            recv_sem=pair_recv.at[k, mask],
            device_id=pair,
            device_id_type=MESH,
        )

    def arrival(k, mask, phase):
        dim = order(phase)[last(mask, phase)]
        here = block(k, mask, core)
        return pltpu.make_async_remote_copy(
            src_ref=here,
            dst_ref=here,
            send_sem=hop_send.at[k, mask],
            recv_sem=hop_recv.at[k, mask],
            device_id=(r, flip(chip, 1 << dim) * 2 + core),
            device_id_type=MESH,
        )

    def pair_arrival(k, mask):
        here = block(k, mask, 1 - core)
        return pltpu.make_async_remote_copy(
            src_ref=here,
            dst_ref=here,
            send_sem=pair_send.at[k, mask],
            recv_sem=pair_recv.at[k, mask],
            device_id=pair,
            device_id_type=MESH,
        )

    def pass_on(k, mask, phase):
        for i in range(last(mask, phase) + 1, dims):
            hop(k, mask, order(phase)[i]).start()
        across(k, mask).start()

    def own(k, phase):
        for t in range(CHUNK_TILES):
            for i in range(rows // TILE_ROWS):
                lines = pl.ds(i * TILE_ROWS, TILE_ROWS)
                j = k * CHUNK_TILES + t
                codes = codes_ref[lines, rows_of(j, HALF)]
                even, odd = lookup(books_ref[map_ref[i, j]], codes)
                left = weights_ref[lines, rows_of(2 * j, LANES)].astype(jnp.float32)
                right = weights_ref[lines, rows_of(2 * j + 1, LANES)].astype(jnp.float32)
                w_even, w_odd = split_pairs(left, right)
                place = pl.ds(pl.multiple_of(c * rows + i * TILE_ROWS, TILE_ROWS), TILE_ROWS)
                errors[k, place, t * HALF : (t + 1) * HALF] = even - w_even
                errors[k, place, pairs + t * HALF : pairs + (t + 1) * HALF] = odd - w_odd
        pass_on(k, 0, phase)

    def product(k):
        slot = lax.rem(k, 2)
        pltpu.make_async_copy(h_in.at[slot], h_in.at[slot], in_sem.at[slot]).wait()

        @pl.when(k >= 2)
        def _():
            for copy in out_copies(k - 2, slot):
                copy.wait()

        step = 64

        def convert(n, carry):
            for parity in range(2):
                high, low = halves(h_in[slot, parity, rows_of(n, step), :])
                place = pl.ds(pl.multiple_of(parity * pairs + n * step, step), step)
                h_high[slot, place, :] = high
                h_low[slot, place, :] = low
            return carry

        lax.fori_loop(0, pairs // step, convert, 0)
        for copy in out_copies(k, slot):
            copy.start()

        @pl.when(k + 2 < chunks)
        def _():
            fetch(k + 2, slot)

        def convert_error(n, carry):
            place = rows_of(n, step)
            high, low = halves(errors[k, place, :])
            e_high[place, :] = high
            e_low[place, :] = low
            return carry

        for mask in range(chips):
            pair_arrival(k, mask).wait_recv()
        lax.fori_loop(0, errors.shape[1] // step, convert_error, 0)
        total = three_products(e_high[...], e_low[...], h_high[slot], h_low[slot])

        @pl.when(k == 0)
        def _():
            part_ref[...] = total

        @pl.when(k > 0)
        def _():
            part_ref[...] += total

    pl.semaphore_wait(barrier, dims + 1)
    own(0, 0)

    def turn(step, carry):
        for u in range(dims):
            t = step * dims + u

            @pl.when(t + 1 < chunks)
            def _():
                own(t + 1, (u + 1) % dims)

            for level in range(1, dims + 1):
                k = t - level + 1
                phase = (u - level + 1) % dims

                @pl.when((k >= 0) & (k < chunks))
                def _():
                    for mask in range(1, chips):
                        if mask.bit_count() == level:
                            arrival(k, mask, phase).wait_recv()
                            pass_on(k, mask, phase)

            k = t - dims

            @pl.when((k >= 0) & (k < chunks))
            def _():
                product(k)

        return carry

    lax.fori_loop(0, -(-(chunks + dims) // dims), turn, 0)
    for k in range(max(0, chunks - 2), chunks):
        for copy in out_copies(k, k % 2):
            copy.wait()

    def drain(k, carry):
        for mask in range(chips):
            across(k, mask).wait_send()
            if mask:
                arrival(k, mask, 0).wait_send()
        return carry

    lax.fori_loop(0, chunks, drain, 0)


def first_product(n_col, tile_map, codes, weights, books, hessian):
    rows, length = weights.shape
    count = hessian.shape[0]
    width = hessian.shape[1] * hessian.shape[2] * hessian.shape[3]
    size = CHUNK_TILES * TILE_COLS
    chunks = count // size
    total_rows = rows * n_col
    chips = n_col // 2
    dma = pltpu.SemaphoreType.DMA
    whole = jax.ShapeDtypeStruct((chunks, size, width), jnp.bfloat16)
    return pl.pallas_call(
        functools.partial(first_kernel, n_col, chunks),
        in_specs=[SMEM, VMEM, VMEM, VMEM, ANY],
        out_specs=[VMEM, ANY, ANY],
        out_shape=[jax.ShapeDtypeStruct((total_rows, width), jnp.float32), whole, whole],
        scratch_shapes=[
            pltpu.VMEM((chunks, total_rows, size), jnp.float32),
            pltpu.VMEM((total_rows, size), jnp.bfloat16),
            pltpu.VMEM((total_rows, size), jnp.bfloat16),
            pltpu.VMEM((2, 2, size // 2, width), jnp.float32),
            pltpu.VMEM((2, size, width), jnp.bfloat16),
            pltpu.VMEM((2, size, width), jnp.bfloat16),
            dma((chunks, chips)),
            dma((chunks, chips)),
            dma((chunks, chips)),
            dma((chunks, chips)),
            dma((2,)),
            dma((2,)),
            dma((2,)),
        ],
        compiler_params=pltpu.CompilerParams(collective_id=1, has_side_effects=True, vmem_limit_bytes=VMEM_BYTES),
        cost_estimate=pl.CostEstimate(flops=6 * total_rows * width * count, bytes_accessed=8 * count * width, transcendentals=0),
        name="first_product",
    )(tile_map, codes, weights, books.reshape(-1, 4, LANES), hessian.reshape(count // 2, 2, width // LANES, 1, LANES))


def next_kernel(place_ref, map_ref, codes_ref, delta_ref, high_ref, low_ref, part_ref, d_high, d_low):
    k = pl.program_id(0)
    down = codes_ref.shape[0] // TILE_ROWS
    pairs = CHUNK_TILES * HALF
    begin = place_ref[0] + k * CHUNK_TILES

    def line(i, carry):
        lines = rows_of(i, TILE_ROWS)
        for t in range(CHUNK_TILES):
            codes = codes_ref[lines, t * HALF : (t + 1) * HALF]
            even, odd = lookup(delta_ref[map_ref[i, begin + t]], codes)
            for part, value in enumerate((even, odd)):
                high, low = halves(value)
                at = part * pairs + t * HALF
                d_high[lines, at : at + HALF] = high
                d_low[lines, at : at + HALF] = low
        return carry

    lax.fori_loop(0, down, line, 0, unroll=2)
    total = three_products(d_high[...], d_low[...], high_ref[0], low_ref[0])

    @pl.when(k == 0)
    def _():
        part_ref[...] = total

    @pl.when(k > 0)
    def _():
        part_ref[...] += total


def next_product(begin, full_map, codes, delta, high, low):
    chunks, size, width = high.shape
    m = codes.shape[0]
    spec = pl.BlockSpec((1, size, width), lambda k: (k, 0, 0))
    return pl.pallas_call(
        next_kernel,
        grid=(chunks,),
        in_specs=[
            SMEM,
            SMEM,
            pl.BlockSpec((m, size // 2), lambda k: (0, k)),
            pl.BlockSpec((delta.shape[0] // 4, 4, LANES), lambda k: (0, 0, 0)),
            spec,
            spec,
        ],
        out_specs=pl.BlockSpec((m, width), lambda k: (0, 0)),
        out_shape=jax.ShapeDtypeStruct((m, width), jnp.float32),
        scratch_shapes=[pltpu.VMEM((m, size), jnp.bfloat16), pltpu.VMEM((m, size), jnp.bfloat16)],
        compiler_params=pltpu.CompilerParams(vmem_limit_bytes=VMEM_BYTES),
        cost_estimate=pl.CostEstimate(flops=6 * m * width * size * chunks, bytes_accessed=4 * size * chunks * width, transcendentals=0),
        name="next_product",
    )(begin, full_map, codes, delta.reshape(-1, 4, LANES), high, low)


def spread_tile(codes, left, right):
    even, odd = split_pairs(left, right)
    values = []
    for x in (even, odd):
        high = x.astype(jnp.bfloat16).astype(jnp.float32)
        values += [high, x - high]
    upper = codes // LOW
    lower = (codes & (LOW - 1)).astype(jnp.float32).astype(jnp.bfloat16)
    eight = lax.broadcasted_iota(jnp.int32, (8, LANES), 0)
    entry = lax.broadcasted_iota(jnp.int32, (LOW, LANES), 0).astype(jnp.float32).astype(jnp.bfloat16)
    one, zero = jnp.bfloat16(1), jnp.bfloat16(0)
    parts, hots = [], []
    for n in range(TILE_ROWS):
        fits = eight == upper[n : n + 1, :]
        part = jnp.concatenate([jnp.where(fits, x[n : n + 1, :], 0.0) for x in values], axis=0)
        parts.append(part.astype(jnp.bfloat16))
        hots.append(jnp.where(entry == lower[n : n + 1, :], one, zero))
    return lax.dot_general(
        jnp.concatenate(parts, axis=1), jnp.concatenate(hots, axis=1), NT, preferred_element_type=jnp.float32
    )


def scatter_kernel(run, gap, place_ref, map_ref, codes_ref, grad_ref, books_ref, sums_ref):
    g = pl.program_id(0)
    rows_here, pairs = codes_ref.shape
    down, across = rows_here // TILE_ROWS, pairs // HALF
    top = g * down
    begin = place_ref[0]
    halves_apart = run % TILE_COLS != 0
    row = lax.broadcasted_iota(jnp.int32, (8, LOW), 0)
    lane = lax.broadcasted_iota(jnp.int32, (TILE_ROWS, LANES), 1)

    @pl.when(g == 0)
    def _():
        sums_ref[...] = jnp.zeros_like(sums_ref)

    def book(i, column):
        return map_ref[top + i, ((column // run) * gap + begin + column % run) // TILE_COLS]

    def add(index, sums):
        even, odd = sums[0:8] + sums[8:16], sums[16:24] + sums[24:32]
        first = jnp.where(row < 4, even, jnp.concatenate([odd[4:8], odd[0:4]], axis=0))
        second = jnp.where(row < 4, jnp.concatenate([even[4:8], even[0:4]], axis=0), odd)
        sums_ref[index, :, 0:LOW] += jnp.concatenate([first, second], axis=0)

    def tile(t, carry):
        i, j = t // across, t % across
        rows = rows_of(i, TILE_ROWS)
        codes = codes_ref[rows, rows_of(j, HALF)]
        left = grad_ref[rows, rows_of(2 * j, LANES)]
        right = grad_ref[rows, rows_of(2 * j + 1, LANES)]
        if halves_apart:
            none = jnp.zeros_like(left)
            add(book(i, j * TILE_COLS), spread_tile(codes, left, none))
            add(book(i, j * TILE_COLS + LANES), spread_tile(codes, none, right))
        else:
            add(book(i, j * TILE_COLS), spread_tile(codes, left, right))
        return carry

    lax.fori_loop(0, down * across, tile, 0, unroll=1 if halves_apart else 4)

    @pl.when(g == pl.num_programs(0) - 1)
    def _():
        count = sums_ref.shape[0]
        groups = LANES // LOW
        step = 16
        size = step * 4

        def squeeze(n, carry):
            x = sums_ref[rows_of(n, step)].reshape(size, groups, LANES)
            total = x[:, 0, :]
            for b in range(1, groups):
                total = total + pltpu.roll(x[:, b, :], b * LOW, 1)
            books_ref[rows_of(n, size), :] = total
            return carry

        lax.fori_loop(0, count // step, squeeze, 0)


def scatter(run, gap, begin, full_map, codes, grad, shape):
    m, n = grad.shape
    block = min(m, 128)
    return pl.pallas_call(
        functools.partial(scatter_kernel, run, gap),
        grid=(m // block,),
        in_specs=[
            SMEM,
            SMEM,
            pl.BlockSpec((block, n // 2), lambda i: (i, 0)),
            pl.BlockSpec((block, n), lambda i: (i, 0)),
        ],
        out_specs=pl.BlockSpec(shape, lambda i: (0, 0)),
        out_shape=jax.ShapeDtypeStruct(shape, jnp.float32),
        scratch_shapes=[pltpu.VMEM((shape[0] // 4, 16, LANES), jnp.float32)],
        compiler_params=pltpu.CompilerParams(vmem_limit_bytes=VMEM_BYTES),
        cost_estimate=pl.CostEstimate(flops=64 * 32 * m * n, bytes_accessed=6 * m * n, transcendentals=0),
        name="scatter",
    )(begin, full_map, codes, grad)


def update_kernel(n_row, n_col, final, grad_ref, books_ref, delta_ref, out_ref, pair_in, pair_sum, chip_in, chip_sum, row_in, *sems):
    r, c = lax.axis_index("row"), lax.axis_index("col")
    chip, core = c // 2, lax.rem(c, 2)
    chips = n_col // 2
    half = grad_ref.shape[0] // 2
    wide = half // chips
    thin = wide // n_row
    pair = (r, chip * 2 + 1 - core)
    others = [lax.rem(chip + d, chips) for d in range(chips)]
    lines = [lax.rem(r + d, n_row) for d in range(n_row)]

    barrier = pltpu.get_barrier_semaphore()
    pl.semaphore_signal(barrier, inc=1, device_id=pair, device_id_type=MESH)
    for d in range(1, chips):
        pl.semaphore_signal(barrier, inc=1, device_id=(r, others[d] * 2 + core), device_id_type=MESH)
    for d in range(1, n_row):
        pl.semaphore_signal(barrier, inc=1, device_id=(lines[d], c), device_id_type=MESH)
    pl.semaphore_wait(barrier, chips + n_row - 1)

    pair_send, pair_recv, chip_send, chip_recv, row_send, row_recv, row_send2, row_recv2, chip_send2, chip_recv2, pair_send2, pair_recv2 = sems

    def send(src, dst, sends, recvs, d, device):
        copy = pltpu.make_async_remote_copy(
            src_ref=src, dst_ref=dst, send_sem=sends.at[d], recv_sem=recvs.at[d], device_id=device, device_id_type=MESH
        )
        copy.start()
        return copy

    def total_of(first, received, copies):
        for d, copy in enumerate(copies, 1):
            copy.wait_recv()
            first = first + received[d]
        return first

    copies = []
    swap = send(grad_ref.at[rows_of(1 - core, half)], pair_in, pair_send, pair_recv, 0, pair)
    swap.wait_recv()
    pair_sum[...] = grad_ref[rows_of(core, half), :] + pair_in[...]
    first = [
        send(pair_sum.at[rows_of(others[d], wide)], chip_in.at[d], chip_send, chip_recv, d, (r, others[d] * 2 + core))
        for d in range(1, chips)
    ]
    chip_sum[...] = total_of(pair_sum[rows_of(chip, wide), :], chip_in, first)
    second = [
        send(chip_sum.at[rows_of(lines[d], thin)], row_in.at[d], row_send, row_recv, d, (lines[d], c))
        for d in range(1, n_row)
    ]
    total = total_of(chip_sum[rows_of(r, thin), :], row_in, second)
    mine = rows_of((core * chips + chip) * n_row + r, thin)
    change = -learn_rate * (2.0 * total)
    if final:
        out_ref[mine, :] = books_ref[mine, :] + (2.0 * delta_ref[mine, :] + change)
    else:
        out_ref[mine, :] = change
    third = [send(out_ref.at[mine], out_ref.at[mine], row_send2, row_recv2, d, (lines[d], c)) for d in range(1, n_row)]
    for copy in third:
        copy.wait_recv()
    piece = rows_of(core * chips + chip, wide)
    fourth = [
        send(out_ref.at[piece], out_ref.at[piece], chip_send2, chip_recv2, d, (r, others[d] * 2 + core))
        for d in range(1, chips)
    ]
    for copy in fourth:
        copy.wait_recv()
    part = rows_of(core, half)
    fifth = send(out_ref.at[part], out_ref.at[part], pair_send2, pair_recv2, 0, pair)
    fifth.wait_recv()
    for copy in [swap, fifth] + first + second + third + fourth:
        copy.wait_send()


def update(n_row, n_col, final, grad, books, delta):
    half = grad.shape[0] // 2
    chips = n_col // 2
    wide = half // chips
    thin = wide // n_row
    dma = pltpu.SemaphoreType.DMA
    sizes = [1, 1, chips, chips, n_row, n_row, n_row, n_row, chips, chips, 1, 1]
    return pl.pallas_call(
        functools.partial(update_kernel, n_row, n_col, final),
        in_specs=[VMEM, VMEM, VMEM],
        out_specs=VMEM,
        out_shape=jax.ShapeDtypeStruct(grad.shape, jnp.float32),
        scratch_shapes=[
            pltpu.VMEM((half, LANES), jnp.float32),
            pltpu.VMEM((half, LANES), jnp.float32),
            pltpu.VMEM((chips, wide, LANES), jnp.float32),
            pltpu.VMEM((wide, LANES), jnp.float32),
            pltpu.VMEM((n_row, thin, LANES), jnp.float32),
        ]
        + [dma((size,)) for size in sizes],
        compiler_params=pltpu.CompilerParams(collective_id=2 if final else 0, has_side_effects=True),
        name="last_update" if final else "update",
    )(grad, books, delta)


def per_device(n_row, n_col, hessian, weights, codes, tile_map, codebooks):
    count, parts, entries = codebooks.shape
    books = codebooks.reshape(count, parts, entries // LANES, LANES).transpose(0, 2, 1, 3).reshape(-1, LANES)
    run = hessian.shape[2] * hessian.shape[3]
    r, c = lax.axis_index("row"), lax.axis_index("col")
    begin_row = jnp.full((1,), r * tile_map.shape[1], jnp.int32)
    begin_col = jnp.full((1,), c * run, jnp.int32)

    full_map = lax.all_gather(lax.all_gather(tile_map, "row", axis=1, tiled=True), "col", axis=0, tiled=True)
    code_piece = lax.all_to_all(codes, "col", split_axis=1, concat_axis=0, tiled=True)
    code_spread = lax.all_gather(code_piece, "row", axis=1, tiled=True)

    grad, high, low = first_product(n_col, tile_map, codes, weights, books, hessian)
    grad, held_codes = lax.optimization_barrier((grad, codes))
    code_plane = lax.all_gather(held_codes, "col", axis=0, tiled=True)
    sums = scatter(run, n_col * run, begin_col, full_map, code_spread, grad, books.shape)
    delta = update(n_row, n_col, False, sums, books, books)
    grad = next_product(begin_row, full_map, code_plane, delta, high, low)
    sums = scatter(run, n_col * run, begin_col, full_map, code_spread, grad, books.shape)
    books = update(n_row, n_col, True, sums, books, delta)
    return books.reshape(count, entries // LANES, parts, LANES).transpose(0, 2, 1, 3).reshape(codebooks.shape)


def solution(mesh):
    placed = (P("row", None, "col", None), P("col", "row"), P("col", "row"), P("col", "row"), P())
    body = functools.partial(per_device, mesh.shape["row"], mesh.shape["col"])
    return jax.shard_map(body, mesh=mesh, in_specs=placed, out_specs=P(), check_vma=False)
```

time: 390 us -> 295 us (0.76)
  Pallas kernels: 300 us -> 241 us
  waiting for transfers between devices: 42.1 us -> 0.06 us
  blocking collectives: 20.4 us -> 36.6 us
  local copies, waits for them, and re-layouts: 7.75 us -> 3.73 us
    pallas_call x9 -> x6, Pallas kernels: 300 us -> 241 us  [the longest x2 62.8 us: scatter(): pl.pallas_call(functools.partial(scatter_kernel, run, gap), grid=(m // bl...]
    all_gather x1, waiting for transfers between devices: 42.1 us -> 0.02 us  [per_device(): code_plane = lax.all_gather(held_codes, 'col', axis=0, tiled=True)]
    all_gather x0 -> x2, blocking collectives: none -> 21.8 us  [the longest x1 12.1 us: per_device(): lax.all_gather(tile_map, 'row', axis=1, tiled=True)]
    all_to_all x1, blocking collectives: 20.4 us -> 14.8 us  [per_device(): lax.all_to_all(codes, 'col', split_axis=1, concat_axis=0, tiled=True)]
  transfers between devices with their start and end apart: 3 -> 2, of which waited for: 1 -> 0; matrix products, arithmetic and copies ran while one was open for 1% -> 0% of each run, Pallas kernels for 41% -> 42%
where the time goes in v1:
time: 295 us
  Pallas kernels  241 us (82%)
  blocking collectives  36.6 us (12%)
  between operations  13.5 us (5%)
  local copies, waits for them, and re-layouts  3.73 us (1%)
    pallas_call x2, Pallas kernels, scatter(): pl.pallas_call(functools.partial(scatter_kernel, run, gap), grid=(m // bl...  62.8 us
    pallas_call x2, Pallas kernels, update(): pl.pallas_call(functools.partial(update_kernel, n_row, n_col, final), in_...  62 us
    pallas_call x1, Pallas kernels, first_product(): pl.pallas_call(functools.partial(first_kernel, n_col, chunks), in_specs=[...  61.7 us
    pallas_call x1, Pallas kernels, next_product(): pl.pallas_call(next_kernel, grid=(chunks,), in_specs=[SMEM, SMEM, pl.Bloc...  54.3 us
    all_to_all x1, blocking collectives, per_device(): lax.all_to_all(codes, 'col', split_axis=1, concat_axis=0, tiled=True)  14.8 us
    all_gather x1, blocking collectives, per_device(): lax.all_gather(tile_map, 'row', axis=1, tiled=True)  12.1 us
    all_gather x1, blocking collectives, per_device(): lax.all_gather(lax.all_gather(tile_map, 'row', axis=1, tiled=True), 'col'...  9.72 us
  transfers between devices with their start and end apart: 2, of which 0 were waited for; matrix products, arithmetic and copies ran while one was open for 0% of the time, Pallas kernels for 42%

profile of v1, /device:TPU:0, one launch (start us, length us, event | category | flops | bytes accessed | tf_op | source)
XLA Modules:
  0.0 294.8 jit_solution(8693090515258125305)
XLA Ops:
  6.5 0.0 all-gather.5.cloned.1.call-start
  6.5 1.1 copy.19
  7.6 14.8 %all_to_all.19 = s32[64,8,256]{2,0,1:T(8,128)} all-to-all(s32[64,8,256]{2,0,1:T(8,128)S(1)} %bitcast.40), channel_id=1, replica_groups=mesh['row'=4,'col'=8] {'col'}, dimensions={1} | all-to-all | bytes 1048576 | tf_op jit(solution)/shard_map/all_to_all | solution.py:572
  22.4 0.0 all-gather.5.cloned.1.call-update
  22.5 0.0 all-gather.7.cloned.1.call-start
  22.5 0.0 copy-start
  22.5 61.7 %first_product.1 = (f32[512,2048]{1,0:T(8,128)}, bf16[8,512,2048]{2,1,0:T(8,128)(2,1)}, bf16[8,512,2048]{2,1,0:T(8,128)(2,1)}) custom-call(s32[4,16]{1,0:T(4,128)} %map_ref.1, s32[64,2048]{1,0:T(8,128)} %codes_ref.1, bf16[64,4096]{1,0:T(8,128)(2,1)} %weights_ref.1, f32[512,4,128]{2,1,0:T(4,128)} %bitcast.32, f32[2048,2,16,1,128]{4,3,2,1,0:T(1,128)} %bitcast.46), custom_call_target="tpu_custom_call" | custom-call | flops 25769803776 | bytes 67108864 | tf_op jit(solution)/shard_map/first_product/pallas_call | solution.py:287
  84.3 0.0 all-gather.7.cloned.1.call-update
  84.3 0.0 copy-done
  84.3 12.1 %all-gather = s32[4,16,4]{1,2,0:T(4,128)S(1)} all-gather(s32[1,16,4]{1,2,0:T(4,128)S(1)} %bitcast.45), channel_id=1, replica_groups=mesh['row'=4,'col'=8] {'row'}, dimensions={0}, use_global_device_ids=true | all-gather | bytes 1280 | tf_op jit(solution)/shard_map/all_gather | solution.py:571
  96.4 0.1 reshape.28
  96.5 9.7 %all-gather.1 = s32[8,4,64]{2,1,0:T(4,128)} all-gather(s32[1,4,64]{2,1,0:T(4,128)S(1)} %bitcast.44), channel_id=1, replica_groups=mesh['row'=4,'col'=8] {'col'}, dimensions={0}, use_global_device_ids=true | all-gather | bytes 9216 | tf_op jit(solution)/shard_map/all_gather | solution.py:571
  106.2 0.0 all-gather.5.cloned.1.call-done.codes_ref
  106.2 31.4 %scatter.2.grad_ref = f32[2048,128]{1,0:T(8,128)} custom-call(s32[1]{0:T(128)} %bitcast.place_ref, s32[32,64]{1,0:T(8,128)} %bitcast.41, s32[512,1024]{1,0:T(8,128)} %all-gather.5.cloned.1.call-done.codes_ref, f32[512,2048]{1,0:T(8,128)} %get-tuple-element.12.grad_ref), custom_call_target="tpu_custom_call" | custom-call | flops 2147483648 | bytes 6291456 | tf_op jit(solution)/shard_map/scatter/pallas_call | solution.py:449
  137.6 31.0 %update.1.delta_ref = f32[2048,128]{1,0:T(8,128)} custom-call(f32[2048,128]{1,0:T(8,128)} %scatter.2.grad_ref, f32[2048,128]{1,0:T(8,128)} %bitcast.33, f32[2048,128]{1,0:T(8,128)} %bitcast.34), custom_call_target="tpu_custom_call" | custom-call | tf_op jit(solution)/shard_map/update/pallas_call | solution.py:545
  168.6 0.0 all-gather.7.cloned.1.call-done.codes_ref
  168.6 54.3 %next_product.1.grad_ref = f32[512,2048]{1,0:T(8,128)} custom-call(s32[1]{0:T(128)} %bitcast.8.place_ref, s32[32,64]{1,0:T(8,128)} %bitcast.42, s32[512,2048]{1,0:T(8,128)} %all-gather.7.cloned.1.call-done.codes_ref, f32[512,4,128]{2,1,0:T(4,128)} %bitcast.37, bf16[8,512,2048]{2,1,0:T(8,128)(2,1)} %get-tuple-element.13.high_ref, ...), custom_call_target="tpu_custom_call" | custom-call | flops 25769803776 | bytes 33554432 | tf_op jit(solution)/shard_map/next_product/pallas_call | solution.py:347
  222.9 31.4 %scatter.3.grad_ref = f32[2048,128]{1,0:T(8,128)} custom-call(s32[1]{0:T(128)} %bitcast.place_ref, s32[32,64]{1,0:T(8,128)} %bitcast.43, s32[512,1024]{1,0:T(8,128)} %all-gather.5.cloned.1.call-done.codes_ref, f32[512,2048]{1,0:T(8,128)} %next_product.1.grad_ref), custom_call_target="tpu_custom_call" | custom-call | flops 2147483648 | bytes 6291456 | tf_op jit(solution)/shard_map/scatter/pallas_call | solution.py:449
  254.3 31.1 %last_update.1 = f32[2048,128]{1,0:T(8,128)} custom-call(f32[2048,128]{1,0:T(8,128)} %scatter.3.grad_ref, f32[2048,128]{1,0:T(8,128)} %bitcast.35, f32[2048,128]{1,0:T(8,128)} %update.1.delta_ref), custom_call_target="tpu_custom_call" | custom-call | tf_op jit(solution)/shard_map/last_update/pallas_call | solution.py:545
  285.4 2.6 copy.21
  (1 shorter events, 0.0 us)
Async XLA Ops:
  6.5 99.7 %all-gather.5.cloned.1.call-start = ((), (), s32[]{:S(2)}) async-start(), calls=%async_computation.1 | async-start | bytes 2621440 | tf_op jit(solution)/shard_map/all_gather | solution.py:573
  22.5 146.1 %all-gather.7.cloned.1.call-start = ((), (), s32[]{:S(2)}) async-start(), calls=%async_computation.2 | async-start | bytes 4718592 | tf_op jit(solution)/shard_map/all_gather | solution.py:577
  22.5 61.8 %copy-start = (s32[4,16]{1,0:T(4,128)S(1)}, s32[4,16]{1,0:T(4,128)}, u32[]{:S(2)}) copy-start(s32[4,16]{1,0:T(4,128)} %map_ref.1) | copy-start | bytes 772
Sparse Core Ops, SparseCore 0:
  22.6 45.0 all-gather.4
  84.4 36.8 all-gather.6

commit v2 on v1

v2 whole, which is shorter than its diff:
```python
import functools

import jax
import jax.numpy as jnp
from jax import lax
from jax.experimental import pallas as pl
from jax.experimental.pallas import tpu as pltpu
from jax.sharding import PartitionSpec as P

TILE_ROWS = 16
TILE_COLS = 256
STEPS = 2
LANES = 128
HALF = TILE_COLS // 2
CHUNK_TILES = 2
LOW = 32

learn_rate = 0.01
MESH = pl.DeviceIdType.MESH
NT = (((1,), (1,)), ((), ()))
VMEM = pl.BlockSpec(memory_space=pltpu.VMEM)
SMEM = pl.BlockSpec(memory_space=pltpu.SMEM)
ANY = pl.BlockSpec(memory_space=pl.ANY)
VMEM_BYTES = 62 * 2**20


def pick(table, index):
    return jnp.take_along_axis(table, index, axis=1, mode="promise_in_bounds")


def lookup(table, code):
    index = code & (LANES - 1)
    upper = code >= LANES
    tables = [jnp.broadcast_to(table[n : n + 1, :], code.shape) for n in range(4)]
    even = jnp.where(upper, pick(tables[2], index), pick(tables[0], index))
    odd = jnp.where(upper, pick(tables[3], index), pick(tables[1], index))
    return even, odd


def split_pairs(left, right):
    lane = lax.broadcasted_iota(jnp.int32, left.shape, 1)
    first = lane < LANES // 2
    index = (2 * lane) & (LANES - 1)
    even = jnp.where(first, pick(left, index), pick(right, index))
    odd = jnp.where(first, pick(left, index + 1), pick(right, index + 1))
    return even, odd


def halves(x):
    high = x.astype(jnp.bfloat16)
    return high, (x - high.astype(jnp.float32)).astype(jnp.bfloat16)


def three_products(a_high, a_low, b_high, b_low):
    dot = functools.partial(jnp.dot, preferred_element_type=jnp.float32)
    return dot(a_high, b_low) + dot(a_low, b_high) + dot(a_high, b_high)


def flip(chip, mask):
    bit = 0
    while mask >> bit:
        if (mask >> bit) & 1:
            size = 1 << bit
            chip = chip + (1 - 2 * lax.rem(chip // size, 2)) * size
        bit += 1
    return chip


def rows_of(index, size):
    return pl.ds(pl.multiple_of(index * size, size), size)


class Cube:
    def __init__(self, n_col, view, first, sems):
        self.r, c = lax.axis_index("row"), lax.axis_index("col")
        self.chip, self.core = c // 2, lax.rem(c, 2)
        self.chips = n_col // 2
        self.dims = self.chips.bit_length() - 1
        self.view, self.first = view, first
        self.hop_send, self.hop_recv, self.pair_send, self.pair_recv = sems

    def order(self, phase):
        return [(phase + i) % self.dims for i in range(self.dims)]

    def last(self, mask, phase):
        return max([i for i, d in enumerate(self.order(phase)) if (mask >> d) & 1], default=-1)

    def block(self, k, mask, core):
        return self.view(k, flip(self.chip, mask) * 2 + core)

    def copy(self, k, mask, target, sends, recvs, device, core):
        here = self.block(k, mask, core)
        return pltpu.make_async_remote_copy(
            src_ref=here if mask or self.first is None else self.first(k),
            dst_ref=here,
            send_sem=sends.at[k, target],
            recv_sem=recvs.at[k, target],
            device_id=device,
            device_id_type=MESH,
        )

    def hop(self, k, mask, target, dim):
        device = (self.r, flip(self.chip, 1 << dim) * 2 + self.core)
        return self.copy(k, mask, target, self.hop_send, self.hop_recv, device, self.core)

    def across(self, k, mask):
        device = (self.r, self.chip * 2 + 1 - self.core)
        return self.copy(k, mask, mask, self.pair_send, self.pair_recv, device, self.core)

    def pass_on(self, k, mask, phase):
        for i in range(self.last(mask, phase) + 1, self.dims):
            dim = self.order(phase)[i]
            self.hop(k, mask, mask | (1 << dim), dim).start()
        self.across(k, mask).start()

    def arrivals(self, k, level, phase):
        for mask in range(1, self.chips):
            if mask.bit_count() == level:
                self.hop(k, mask, mask, self.order(phase)[self.last(mask, phase)]).wait_recv()
                self.pass_on(k, mask, phase)

    def pair_arrivals(self, k):
        device = (self.r, self.chip * 2 + 1 - self.core)
        for mask in range(self.chips):
            self.copy(k, mask, mask, self.pair_send, self.pair_recv, device, 1 - self.core).wait_recv()

    def drain(self, chunks):
        def one(k, carry):
            for mask in range(self.chips):
                self.across(k, mask).wait_send()
                if mask:
                    self.hop(k, mask, mask, 0).wait_send()
            return carry

        lax.fori_loop(0, chunks, one, 0)

    def turns(self, chunks, extra, begin, work):
        unroll = self.dims * (1 + self.dims % 2)
        count = chunks + self.dims + extra

        def turn(step, carry):
            for u in range(unroll):
                t = step * unroll + u

                @pl.when(t + 1 < chunks)
                def _():
                    begin(t + 1, u + 1)

                for level in range(1, self.dims + 1):
                    k = t - level + 1

                    @pl.when((k >= 0) & (k < chunks))
                    def _():
                        self.arrivals(k, level, (u - level + 1) % self.dims)

                work(t - self.dims, (u - self.dims) % 2)
            return carry

        lax.fori_loop(0, -(-count // unroll), turn, 0)


def greet(devices):
    barrier = pltpu.get_barrier_semaphore()
    for device in devices:
        pl.semaphore_signal(barrier, inc=1, device_id=device, device_id_type=MESH)
    pl.semaphore_wait(barrier, len(devices))


def first_kernel(n_row, n_col, chunks, run, map_ref, padded_ref, codes_ref, weights_ref, books_ref, hessian_ref, part_ref, high_out, low_out, spread_out, maps_out, errors, e_high, e_low, h_in, high0, high1, low0, low1, hop_send, hop_recv, pair_send, pair_recv, in_sem, out_sem, code_send, code_recv, own_sem, line_send, line_recv, map_send, map_recv, map_send2, map_recv2):
    r, c = lax.axis_index("row"), lax.axis_index("col")
    rows = codes_ref.shape[0]
    width = h_in.shape[3]
    pairs = CHUNK_TILES * HALF
    h_high, h_low = (high0, high1), (low0, low1)
    cols = [lax.rem(c + d, n_col) for d in range(n_col)]
    lines = [lax.rem(r + d, n_row) for d in range(n_row)]
    cube = Cube(n_col, lambda k, at: errors.at[k, rows_of(at, rows)], None, (hop_send, hop_recv, pair_send, pair_recv))

    def fetch(k, slot):
        def one(n, carry):
            for parity in range(2):
                pltpu.make_async_copy(
                    hessian_ref.at[rows_of(k, pairs), parity, n, 0],
                    h_in.at[slot, parity, :, rows_of(n, LANES)],
                    in_sem.at[slot],
                ).start()
            return carry

        lax.fori_loop(0, width // LANES, one, 0)

    def fetched(slot):
        pltpu.make_async_copy(h_in.at[slot], h_in.at[slot], in_sem.at[slot]).wait()

    def out_copies(k, slot):
        return [
            pltpu.make_async_copy(h_high[slot], high_out.at[k], out_sem.at[slot, 0]),
            pltpu.make_async_copy(h_low[slot], low_out.at[k], out_sem.at[slot, 1]),
        ]

    def convert(slot, columns):
        for parity in range(2):
            high, low = halves(h_in[slot, parity, :, columns])
            h_high[slot][parity * pairs : (parity + 1) * pairs, columns] = high
            h_low[slot][parity * pairs : (parity + 1) * pairs, columns] = low

    fetch(0, 0)
    if chunks > 1:
        fetch(1, 1)
    part_ref[...] = jnp.zeros_like(part_ref)
    maps_out[r, c] = padded_ref[...]
    greet([(r, cols[d]) for d in range(1, n_col)] + [(lines[d], c) for d in range(1, n_row)])

    span = max(run // 2, LANES)

    def piece(at):
        return codes_ref.at[:, rows_of(at * (run // 2) // span, span)]

    def send(src, dst, sends, recvs, d, device):
        return pltpu.make_async_remote_copy(
            src_ref=src, dst_ref=dst, send_sem=sends.at[d], recv_sem=recvs.at[d], device_id=device, device_id_type=MESH
        )

    here = spread_out.at[r, rows_of(c, rows)]
    spreads = [send(piece(cols[d]), here, code_send, code_recv, d, (r, cols[d])) for d in range(1, n_col)]
    maps = [send(padded_ref, maps_out.at[r, c], map_send, map_recv, d, (r, cols[d])) for d in range(1, n_col)]
    map_lines = [send(maps_out.at[r], maps_out.at[r], map_send2, map_recv2, d, (lines[d], c)) for d in range(1, n_row)]
    keep = pltpu.make_async_copy(piece(c), here, own_sem)

    def along(at, way):
        return pltpu.make_async_remote_copy(
            src_ref=spread_out.at[at],
            dst_ref=spread_out.at[at],
            send_sem=line_send.at[way, at],
            recv_sem=line_recv.at[way, at],
            device_id=(r + 1 - 2 * way, c),
            device_id_type=MESH,
        )

    def lines_start():
        for copy in maps + spreads:
            copy.wait_recv()
        keep.wait()
        for copy in map_lines:
            copy.start()

        @pl.when(r + 1 < n_row)
        def _():
            along(r, 0).start()

        @pl.when(r > 0)
        def _():
            along(r, 1).start()

    def lines_pass(d):
        @pl.when(r >= d)
        def _():
            along(r - d, 0).wait_recv()

            @pl.when(r + 1 < n_row)
            def _():
                along(r - d, 0).start()

        @pl.when(r + d < n_row)
        def _():
            along(r + d, 1).wait_recv()

            @pl.when(r > 0)
            def _():
                along(r + d, 1).start()

    def lines_drain():
        for copy in map_lines:
            copy.wait_recv()
        for copy in maps + spreads + map_lines:
            copy.wait_send()
        for d in range(n_row):
            @pl.when((r >= d) & (r + 1 < n_row))
            def _():
                along(r - d, 0).wait_send()

            @pl.when((r + d < n_row) & (r > 0))
            def _():
                along(r + d, 1).wait_send()

    def own(k, phase):
        for t in range(CHUNK_TILES):
            for i in range(rows // TILE_ROWS):
                at = pl.ds(i * TILE_ROWS, TILE_ROWS)
                j = k * CHUNK_TILES + t
                codes = codes_ref[at, rows_of(j, HALF)]
                even, odd = lookup(books_ref[map_ref[i, j]], codes)
                left = weights_ref[at, rows_of(2 * j, LANES)].astype(jnp.float32)
                right = weights_ref[at, rows_of(2 * j + 1, LANES)].astype(jnp.float32)
                w_even, w_odd = split_pairs(left, right)
                place = pl.ds(pl.multiple_of(c * rows + i * TILE_ROWS, TILE_ROWS), TILE_ROWS)
                errors[k, place, t * HALF : (t + 1) * HALF] = even - w_even
                errors[k, place, pairs + t * HALF : pairs + (t + 1) * HALF] = odd - w_odd
        cube.pass_on(k, 0, phase)

    nt = min(width, 512)

    def multiply(slot, columns):
        part_ref[:, columns] += three_products(e_high[...], e_low[...], h_high[slot][:, columns], h_low[slot][:, columns])

    def product(k, slot):
        step = 64

        @pl.when((k >= 0) & (k < chunks))
        def _():
            cube.pair_arrivals(k)

            def convert_error(n, carry):
                place = rows_of(n, step)
                e_high[place, :], e_low[place, :] = halves(errors[k, place, :])
                return carry

            lax.fori_loop(0, errors.shape[1] // step, convert_error, 0)

        @pl.when((k >= 0) & (k + 1 < chunks))
        def _():
            fetched(1 - slot)

            @pl.when(k >= 1)
            def _():
                for copy in out_copies(k - 1, 1 - slot):
                    copy.wait()

            def both(n, carry):
                columns = rows_of(n, nt)
                multiply(slot, columns)
                convert(1 - slot, columns)
                return carry

            lax.fori_loop(0, width // nt, both, 0)
            for copy in out_copies(k + 1, 1 - slot):
                copy.start()

            @pl.when(k + 3 < chunks)
            def _():
                fetch(k + 3, 1 - slot)

        @pl.when(k + 1 == chunks)
        def _():
            def alone(n, carry):
                multiply(slot, rows_of(n, nt))
                return carry

            lax.fori_loop(0, width // nt, alone, 0)

        @pl.when(k == 0)
        def _():
            lines_start()

        for d in range(1, n_row):
            @pl.when(k == min(2 * d, chunks - 1))
            def _():
                lines_pass(d)

    for copy in spreads + maps + [keep]:
        copy.start()
    own(0, 0)
    fetched(0)

    def convert_first(n, carry):
        convert(0, rows_of(n, nt))
        return carry

    lax.fori_loop(0, width // nt, convert_first, 0)
    for copy in out_copies(0, 0):
        copy.start()
    if chunks > 2:
        fetch(2, 0)

    cube.turns(chunks, 0, own, product)
    for k in range(max(0, chunks - 2), chunks):
        for copy in out_copies(k, k % 2):
            copy.wait()
    lines_drain()
    cube.drain(chunks)


def first_product(n_row, n_col, tile_map, padded, codes, weights, books, hessian):
    rows, length = weights.shape
    count = hessian.shape[0]
    run = hessian.shape[2] * hessian.shape[3]
    width = hessian.shape[1] * run
    size = CHUNK_TILES * TILE_COLS
    chunks = count // size
    total_rows = rows * n_col
    chips = n_col // 2
    dma = pltpu.SemaphoreType.DMA
    whole = jax.ShapeDtypeStruct((chunks, size, width), jnp.bfloat16)
    block = pltpu.VMEM((size, width), jnp.bfloat16)
    return pl.pallas_call(
        functools.partial(first_kernel, n_row, n_col, chunks, run),
        in_specs=[SMEM, VMEM, VMEM, VMEM, VMEM, ANY],
        out_specs=[VMEM, ANY, ANY, ANY, VMEM],
        out_shape=[
            jax.ShapeDtypeStruct((total_rows, width), jnp.float32),
            whole,
            whole,
            jax.ShapeDtypeStruct((n_row, total_rows, max(run // 2, LANES)), jnp.int32),
            jax.ShapeDtypeStruct((n_row, n_col) + padded.shape, jnp.int32),
        ],
        scratch_shapes=[
            pltpu.VMEM((chunks, total_rows, size), jnp.float32),
            pltpu.VMEM((total_rows, size), jnp.bfloat16),
            pltpu.VMEM((total_rows, size), jnp.bfloat16),
            pltpu.VMEM((2, 2, size // 2, width), jnp.float32),
            block,
            block,
            block,
            block,
            dma((chunks, chips)),
            dma((chunks, chips)),
            dma((chunks, chips)),
            dma((chunks, chips)),
            dma((2,)),
            dma((2, 2)),
            dma((n_col,)),
            dma((n_col,)),
            dma,
            dma((2, n_row)),
            dma((2, n_row)),
            dma((n_col,)),
            dma((n_col,)),
            dma((n_row,)),
            dma((n_row,)),
        ],
        compiler_params=pltpu.CompilerParams(collective_id=1, has_side_effects=True, vmem_limit_bytes=VMEM_BYTES),
        cost_estimate=pl.CostEstimate(flops=6 * total_rows * width * count, bytes_accessed=8 * count * width, transcendentals=0),
        name="first_product",
    )(tile_map, padded, codes, weights, books.reshape(-1, 4, LANES), hessian.reshape(count // 2, 2, width // LANES, 1, LANES))


def next_kernel(n_col, chunks, down, map_ref, codes_ref, delta_ref, high_ref, low_ref, part_ref, codes_all, high0, high1, low0, low1, d_high0, d_high1, d_low0, d_low1, hop_send, hop_recv, pair_send, pair_recv, in_sem):
    r, c = lax.axis_index("row"), lax.axis_index("col")
    rows = codes_ref.shape[0]
    total_rows, width = part_ref.shape
    pairs = CHUNK_TILES * HALF
    h_high, h_low = (high0, high1), (low0, low1)
    d_high, d_low = (d_high0, d_high1), (d_low0, d_low1)
    cube = Cube(
        n_col,
        lambda k, at: codes_all.at[k, rows_of(at, rows)],
        lambda k: codes_ref.at[:, rows_of(k, pairs)],
        (hop_send, hop_recv, pair_send, pair_recv),
    )

    def fetch(k, slot):
        return [
            pltpu.make_async_copy(high_ref.at[k], h_high[slot], in_sem.at[slot, 0]),
            pltpu.make_async_copy(low_ref.at[k], h_low[slot], in_sem.at[slot, 1]),
        ]

    for k in range(min(2, chunks)):
        for copy in fetch(k, k):
            copy.start()
    part_ref[...] = jnp.zeros_like(part_ref)
    greet(
        [(r, flip(cube.chip, 1 << d) * 2 + cube.core) for d in range(cube.dims)] + [(r, cube.chip * 2 + 1 - cube.core)]
    )

    def own(k, phase):
        cube.pass_on(k, 0, phase)
        codes_all[k, rows_of(c, rows), :] = codes_ref[:, rows_of(k, pairs)]

    nt = min(width, 512)
    tiles = total_rows // TILE_ROWS
    share = tiles // (width // nt)

    def look(k, slot, n):
        for q in range(share):
            i = n * share + q
            at = rows_of(i, TILE_ROWS)
            for t in range(CHUNK_TILES):
                codes = codes_all[k, at, t * HALF : (t + 1) * HALF]
                book = map_ref[r, i // down, lax.rem(i, down), k * CHUNK_TILES + t]
                for part, value in enumerate(lookup(delta_ref[book], codes)):
                    high, low = halves(value)
                    left = part * pairs + t * HALF
                    d_high[slot][at, left : left + HALF] = high
                    d_low[slot][at, left : left + HALF] = low

    def multiply(slot, n):
        columns = rows_of(n, nt)
        part_ref[:, columns] += three_products(
            d_high[slot][...], d_low[slot][...], h_high[slot][:, columns], h_low[slot][:, columns]
        )

    def loop(body):
        def one(n, carry):
            body(n)
            return carry

        lax.fori_loop(0, width // nt, one, 0)

    def work(k, slot):
        @pl.when((k >= 0) & (k < chunks))
        def _():
            cube.pair_arrivals(k)

        @pl.when((k >= 1) & (k <= chunks))
        def _():
            for copy in fetch(k - 1, 1 - slot):
                copy.wait()

        @pl.when(k == 0)
        def _():
            loop(lambda n: look(k, slot, n))

        @pl.when((k >= 1) & (k < chunks))
        def _():
            def body(n):
                multiply(1 - slot, n)
                look(k, slot, n)

            loop(body)

        @pl.when(k == chunks)
        def _():
            loop(lambda n: multiply(1 - slot, n))

        @pl.when((k >= 1) & (k + 1 < chunks))
        def _():
            for copy in fetch(k + 1, 1 - slot):
                copy.start()

    own(0, 0)
    cube.turns(chunks, 1, own, work)
    cube.drain(chunks)


def next_product(n_col, down, maps, codes, delta, high, low):
    chunks, size, width = high.shape
    rows = codes.shape[0]
    m = rows * n_col
    chips = n_col // 2
    dma = pltpu.SemaphoreType.DMA
    block = pltpu.VMEM((size, width), jnp.bfloat16)
    factor = pltpu.VMEM((m, size), jnp.bfloat16)
    return pl.pallas_call(
        functools.partial(next_kernel, n_col, chunks, down),
        in_specs=[SMEM, VMEM, VMEM, ANY, ANY],
        out_specs=VMEM,
        out_shape=jax.ShapeDtypeStruct((m, width), jnp.float32),
        scratch_shapes=[pltpu.VMEM((chunks, m, size // 2), jnp.int32)]
        + [block] * 4
        + [factor] * 4
        + [dma((chunks, chips))] * 4
        + [dma((2, 2))],
        compiler_params=pltpu.CompilerParams(collective_id=3, has_side_effects=True, vmem_limit_bytes=VMEM_BYTES),
        cost_estimate=pl.CostEstimate(flops=6 * m * width * size * chunks, bytes_accessed=4 * size * chunks * width, transcendentals=0),
        name="next_product",
    )(maps, codes, delta.reshape(-1, 4, LANES), high, low)


def spread_tile(codes, left, right):
    even, odd = split_pairs(left, right)
    values = []
    for x in (even, odd):
        high = x.astype(jnp.bfloat16).astype(jnp.float32)
        values += [high, x - high]
    upper = codes // LOW
    lower = (codes & (LOW - 1)).astype(jnp.float32).astype(jnp.bfloat16)
    eight = lax.broadcasted_iota(jnp.int32, (8, LANES), 0)
    entry = lax.broadcasted_iota(jnp.int32, (LOW, LANES), 0).astype(jnp.float32).astype(jnp.bfloat16)
    one, zero = jnp.bfloat16(1), jnp.bfloat16(0)
    parts, hots = [], []
    for n in range(TILE_ROWS):
        fits = eight == upper[n : n + 1, :]
        part = jnp.concatenate([jnp.where(fits, x[n : n + 1, :], 0.0) for x in values], axis=0)
        parts.append(part.astype(jnp.bfloat16))
        hots.append(jnp.where(entry == lower[n : n + 1, :], one, zero))
    return lax.dot_general(
        jnp.concatenate(parts, axis=1), jnp.concatenate(hots, axis=1), NT, preferred_element_type=jnp.float32
    )


def scatter_kernel(run, gap, sizes, place_ref, map_ref, codes_ref, grad_ref, books_ref, sums_ref):
    g = pl.program_id(0)
    groups, rows_here, span = codes_ref.shape
    down, across = rows_here // TILE_ROWS, groups * span // HALF
    map_down, map_across = sizes
    top = g * down
    begin = place_ref[0]
    halves_apart = run % TILE_COLS != 0
    row = lax.broadcasted_iota(jnp.int32, (8, LOW), 0)

    @pl.when(g == 0)
    def _():
        sums_ref[...] = jnp.zeros_like(sums_ref)

    def book(i, column):
        line = top + i
        tile = ((column // run) * gap + begin + column % run) // TILE_COLS
        return map_ref[tile // map_across, line // map_down, line % map_down, tile % map_across]

    def add(index, sums):
        even, odd = sums[0:8] + sums[8:16], sums[16:24] + sums[24:32]
        first = jnp.where(row < 4, even, jnp.concatenate([odd[4:8], odd[0:4]], axis=0))
        second = jnp.where(row < 4, jnp.concatenate([even[4:8], even[0:4]], axis=0), odd)
        sums_ref[index, :, 0:LOW] += jnp.concatenate([first, second], axis=0)

    def tile(t, carry):
        i, j = t // across, t % across
        rows = rows_of(i, TILE_ROWS)
        codes = codes_ref[j // (span // HALF), rows, rows_of(j % (span // HALF), HALF)]
        left = grad_ref[rows, rows_of(2 * j, LANES)]
        right = grad_ref[rows, rows_of(2 * j + 1, LANES)]
        if halves_apart:
            none = jnp.zeros_like(left)
            add(book(i, j * TILE_COLS), spread_tile(codes, left, none))
            add(book(i, j * TILE_COLS + LANES), spread_tile(codes, none, right))
        else:
            add(book(i, j * TILE_COLS), spread_tile(codes, left, right))
        return carry

    lax.fori_loop(0, down * across, tile, 0, unroll=1 if halves_apart else 4)

    @pl.when(g == pl.num_programs(0) - 1)
    def _():
        count = sums_ref.shape[0]
        groups = LANES // LOW
        step = 16
        size = step * 4

        def squeeze(n, carry):
            x = sums_ref[rows_of(n, step)].reshape(size, groups, LANES)
            total = x[:, 0, :]
            for b in range(1, groups):
                total = total + pltpu.roll(x[:, b, :], b * LOW, 1)
            books_ref[rows_of(n, size), :] = total
            return carry

        lax.fori_loop(0, count // step, squeeze, 0)


def scatter(run, gap, sizes, begin, maps, codes, grad, shape):
    m, n = grad.shape
    block = min(m, 128)
    return pl.pallas_call(
        functools.partial(scatter_kernel, run, gap, sizes),
        grid=(m // block,),
        in_specs=[
            SMEM,
            SMEM,
            pl.BlockSpec((codes.shape[0], block, codes.shape[2]), lambda i: (0, i, 0)),
            pl.BlockSpec((block, n), lambda i: (i, 0)),
        ],
        out_specs=pl.BlockSpec(shape, lambda i: (0, 0)),
        out_shape=jax.ShapeDtypeStruct(shape, jnp.float32),
        scratch_shapes=[pltpu.VMEM((shape[0] // 4, 16, LANES), jnp.float32)],
        compiler_params=pltpu.CompilerParams(vmem_limit_bytes=VMEM_BYTES),
        cost_estimate=pl.CostEstimate(flops=64 * 32 * m * n, bytes_accessed=6 * m * n, transcendentals=0),
        name="scatter",
    )(begin, maps, codes, grad)


def update_kernel(n_row, n_col, final, grad_ref, books_ref, delta_ref, out_ref, pair_in, pair_sum, chip_in, chip_sum, row_in, *sems):
    r, c = lax.axis_index("row"), lax.axis_index("col")
    chip, core = c // 2, lax.rem(c, 2)
    chips = n_col // 2
    half = grad_ref.shape[0] // 2
    wide = half // chips
    thin = wide // n_row
    pair = (r, chip * 2 + 1 - core)
    others = [lax.rem(chip + d, chips) for d in range(chips)]
    lines = [lax.rem(r + d, n_row) for d in range(n_row)]

    barrier = pltpu.get_barrier_semaphore()
    pl.semaphore_signal(barrier, inc=1, device_id=pair, device_id_type=MESH)
    for d in range(1, chips):
        pl.semaphore_signal(barrier, inc=1, device_id=(r, others[d] * 2 + core), device_id_type=MESH)
    for d in range(1, n_row):
        pl.semaphore_signal(barrier, inc=1, device_id=(lines[d], c), device_id_type=MESH)
    pl.semaphore_wait(barrier, chips + n_row - 1)

    pair_send, pair_recv, chip_send, chip_recv, row_send, row_recv, row_send2, row_recv2, chip_send2, chip_recv2, pair_send2, pair_recv2 = sems

    def send(src, dst, sends, recvs, d, device):
        copy = pltpu.make_async_remote_copy(
            src_ref=src, dst_ref=dst, send_sem=sends.at[d], recv_sem=recvs.at[d], device_id=device, device_id_type=MESH
        )
        copy.start()
        return copy

    def total_of(first, received, copies):
        for d, copy in enumerate(copies, 1):
            copy.wait_recv()
            first = first + received[d]
        return first

    copies = []
    swap = send(grad_ref.at[rows_of(1 - core, half)], pair_in, pair_send, pair_recv, 0, pair)
    swap.wait_recv()
    pair_sum[...] = grad_ref[rows_of(core, half), :] + pair_in[...]
    first = [
        send(pair_sum.at[rows_of(others[d], wide)], chip_in.at[d], chip_send, chip_recv, d, (r, others[d] * 2 + core))
        for d in range(1, chips)
    ]
    chip_sum[...] = total_of(pair_sum[rows_of(chip, wide), :], chip_in, first)
    second = [
        send(chip_sum.at[rows_of(lines[d], thin)], row_in.at[d], row_send, row_recv, d, (lines[d], c))
        for d in range(1, n_row)
    ]
    total = total_of(chip_sum[rows_of(r, thin), :], row_in, second)
    mine = rows_of((core * chips + chip) * n_row + r, thin)
    change = -learn_rate * (2.0 * total)
    if final:
        out_ref[mine, :] = books_ref[mine, :] + (2.0 * delta_ref[mine, :] + change)
    else:
        out_ref[mine, :] = change
    third = [send(out_ref.at[mine], out_ref.at[mine], row_send2, row_recv2, d, (lines[d], c)) for d in range(1, n_row)]
    for copy in third:
        copy.wait_recv()
    piece = rows_of(core * chips + chip, wide)
    fourth = [
        send(out_ref.at[piece], out_ref.at[piece], chip_send2, chip_recv2, d, (r, others[d] * 2 + core))
        for d in range(1, chips)
    ]
    for copy in fourth:
        copy.wait_recv()
    part = rows_of(core, half)
    fifth = send(out_ref.at[part], out_ref.at[part], pair_send2, pair_recv2, 0, pair)
    fifth.wait_recv()
    for copy in [swap, fifth] + first + second + third + fourth:
        copy.wait_send()


def update(n_row, n_col, final, grad, books, delta):
    half = grad.shape[0] // 2
    chips = n_col // 2
    wide = half // chips
    thin = wide // n_row
    dma = pltpu.SemaphoreType.DMA
    sizes = [1, 1, chips, chips, n_row, n_row, n_row, n_row, chips, chips, 1, 1]
    return pl.pallas_call(
        functools.partial(update_kernel, n_row, n_col, final),
        in_specs=[VMEM, VMEM, VMEM],
        out_specs=VMEM,
        out_shape=jax.ShapeDtypeStruct(grad.shape, jnp.float32),
        scratch_shapes=[
            pltpu.VMEM((half, LANES), jnp.float32),
            pltpu.VMEM((half, LANES), jnp.float32),
            pltpu.VMEM((chips, wide, LANES), jnp.float32),
            pltpu.VMEM((wide, LANES), jnp.float32),
            pltpu.VMEM((n_row, thin, LANES), jnp.float32),
        ]
        + [dma((size,)) for size in sizes],
        compiler_params=pltpu.CompilerParams(collective_id=2 if final else 0, has_side_effects=True),
        name="last_update" if final else "update",
    )(grad, books, delta)


def per_device(n_row, n_col, hessian, weights, codes, tile_map, codebooks):
    count, parts, entries = codebooks.shape
    books = codebooks.reshape(count, parts, entries // LANES, LANES).transpose(0, 2, 1, 3).reshape(-1, LANES)
    run = hessian.shape[2] * hessian.shape[3]
    c = lax.axis_index("col")
    begin = jnp.full((1,), c * run, jnp.int32)
    down, across = tile_map.shape
    padded = jnp.pad(tile_map, ((0, -down % 8), (0, -across % LANES)))

    grad, high, low, spread, maps = first_product(n_row, n_col, tile_map, padded, codes, weights, books, hessian)
    if run // 2 < spread.shape[2]:
        groups, m, span = spread.shape
        spread = lax.dynamic_slice(spread, (0, 0, lax.rem(c * (run // 2), span)), (groups, m, run // 2))
        spread = spread.transpose(1, 0, 2).reshape(1, m, groups * (run // 2))
    split = functools.partial(scatter, run, n_col * run, (down, across), begin, maps, spread)
    delta = update(n_row, n_col, False, split(grad, books.shape), books, books)
    grad = next_product(n_col, down, maps, codes, delta, high, low)
    books = update(n_row, n_col, True, split(grad, books.shape), books, delta)
    return books.reshape(count, entries // LANES, parts, LANES).transpose(0, 2, 1, 3).reshape(codebooks.shape)


def solution(mesh):
    placed = (P("row", None, "col", None), P("col", "row"), P("col", "row"), P("col", "row"), P())
    body = functools.partial(per_device, mesh.shape["row"], mesh.shape["col"])
    return jax.shard_map(body, mesh=mesh, in_specs=placed, out_specs=P(), check_vma=False)
```

time: 295 us -> 263 us (0.89)
  blocking collectives: 36.6 us -> 0 us
  Pallas kernels: 241 us -> 259 us
  between operations: 13.5 us -> 0.03 us
    all_gather x2 -> x0, blocking collectives: 21.8 us -> none  [the longest x1 12.1 us: per_device(): lax.all_gather(tile_map, 'row', axis=1, tiled=True)]
    pallas_call x4, Pallas kernels: 179 us -> 197 us  [the longest x1 79.8 us: first_product(): pl.pallas_call(functools.partial(first_kernel, n_row, n_col, chunks, run)...]
    all_to_all x1 -> x0, blocking collectives: 14.8 us -> none  [per_device(): lax.all_to_all(codes, 'col', split_axis=1, concat_axis=0, tiled=True)]
  transfers between devices with their start and end apart: 2 -> 0, of which waited for: 0 -> 0; matrix products, arithmetic and copies ran while one was open for 0% -> 0% of each run, Pallas kernels for 42% -> 0%
where the time goes in v2:
time: 263 us
  Pallas kernels  259 us (98%)
  local copies, waits for them, and re-layouts  3.83 us (1%)
    pallas_call x1, Pallas kernels, first_product(): pl.pallas_call(functools.partial(first_kernel, n_row, n_col, chunks, run)...  79.8 us
    pallas_call x2, Pallas kernels, scatter(): pl.pallas_call(functools.partial(scatter_kernel, run, gap, sizes), grid=(...  66 us
    pallas_call x2, Pallas kernels, update(): pl.pallas_call(functools.partial(update_kernel, n_row, n_col, final), in_...  62.8 us
    pallas_call x1, Pallas kernels, next_product(): pl.pallas_call(functools.partial(next_kernel, n_col, chunks, down), in_sp...  50.6 us

profile of v2, /device:TPU:0, one launch (start us, length us, event | category | flops | bytes accessed | tf_op | source)
XLA Modules:
  0.0 263.2 jit_solution(104638143344237754)
XLA Ops:
  0.0 1.3 pad.4.padded_ref
  1.3 79.8 %first_product.1 = (f32[512,2048]{1,0:T(8,128)}, bf16[8,512,2048]{2,1,0:T(8,128)(2,1)}, bf16[8,512,2048]{2,1,0:T(8,128)(2,1)}, s32[4,512,256]{2,1,0:T(8,128)}, s32[4,8,8,128]{3,2,1,0:T(8,128)}) custom-call(s32[4,16]{1,0:T(4,128)} %map_ref.1, s32[8,128]{1,0:T(8,128)} %pad.4.padded_ref, s32[64,2048]{1,0:T(8,128)} %codes_ref.3, bf16[64,4096]{1,0:T(8,128)(2,1)} %weights_ref.1, ...), custom_call_target="tpu_custom_call" | custom-call | flops 25769803776 | bytes 67108864 | tf_op jit(solution)/shard_map/first_product/pallas_call | solution.py:394
  81.1 33.0 %scatter.2.grad_ref = f32[2048,128]{1,0:T(8,128)} custom-call(s32[1]{0:T(128)} %bitcast.place_ref, s32[4,8,8,128]{3,2,1,0:T(8,128)} %get-tuple-element.10.map_ref, s32[4,512,256]{2,1,0:T(8,128)} %get-tuple-element.11.codes_ref, f32[512,2048]{1,0:T(8,128)} %get-tuple-element.12.grad_ref), custom_call_target="tpu_custom_call" | custom-call | flops 2147483648 | bytes 6291456 | tf_op jit(solution)/shard_map/scatter/pallas_call | solution.py:642
  114.1 31.4 %update.1.delta_ref = f32[2048,128]{1,0:T(8,128)} custom-call(f32[2048,128]{1,0:T(8,128)} %scatter.2.grad_ref, f32[2048,128]{1,0:T(8,128)} %bitcast.16, f32[2048,128]{1,0:T(8,128)} %bitcast.17), custom_call_target="tpu_custom_call" | custom-call | tf_op jit(solution)/shard_map/update/pallas_call | solution.py:738
  145.5 50.6 %next_product.1.grad_ref = f32[512,2048]{1,0:T(8,128)} custom-call(s32[4,8,8,128]{3,2,1,0:T(8,128)} %get-tuple-element.10.map_ref, s32[64,2048]{1,0:T(8,128)} %codes_ref.3, f32[512,4,128]{2,1,0:T(4,128)} %bitcast.20, bf16[8,512,2048]{2,1,0:T(8,128)(2,1)} %get-tuple-element.13.high_ref, bf16[8,512,2048]{2,1,0:T(8,128)(2,1)} %get-tuple-element.14.low_ref), custom_call_target="tpu_custom_call" | custom-call | flops 25769803776 | bytes 33554432 | tf_op jit(solution)/shard_map/next_product/pallas_call | solution.py:542
  196.2 33.0 %scatter.3.grad_ref = f32[2048,128]{1,0:T(8,128)} custom-call(s32[1]{0:T(128)} %bitcast.place_ref, s32[4,8,8,128]{3,2,1,0:T(8,128)} %get-tuple-element.10.map_ref, s32[4,512,256]{2,1,0:T(8,128)} %get-tuple-element.11.codes_ref, f32[512,2048]{1,0:T(8,128)} %next_product.1.grad_ref), custom_call_target="tpu_custom_call" | custom-call | flops 2147483648 | bytes 6291456 | tf_op jit(solution)/shard_map/scatter/pallas_call | solution.py:642
  229.2 31.4 %last_update.1 = f32[2048,128]{1,0:T(8,128)} custom-call(f32[2048,128]{1,0:T(8,128)} %scatter.3.grad_ref, f32[2048,128]{1,0:T(8,128)} %bitcast.18, f32[2048,128]{1,0:T(8,128)} %update.1.delta_ref), custom_call_target="tpu_custom_call" | custom-call | tf_op jit(solution)/shard_map/last_update/pallas_call | solution.py:738
  260.6 2.6 copy.9

commit v3 on v2

--- a/solution.py
+++ b/solution.py
@@ -14,6 +14,7 @@
 HALF = TILE_COLS // 2
 CHUNK_TILES = 2
 LOW = 32
+PARTS = 2
 
 learn_rate = 0.01
 MESH = pl.DeviceIdType.MESH
@@ -134,24 +135,27 @@
 
         lax.fori_loop(0, chunks, one, 0)
 
-    def turns(self, chunks, extra, begin, work):
+    def turns(self, chunks, extra, ahead, begin, work, prepare=lambda: None):
         unroll = self.dims * (1 + self.dims % 2)
         count = chunks + self.dims + extra
+        for k in range(min(ahead, chunks)):
+            begin(k, k)
+        prepare()
 
         def turn(step, carry):
             for u in range(unroll):
                 t = step * unroll + u
 
-                @pl.when(t + 1 < chunks)
-                def _():
-                    begin(t + 1, u + 1)
-
-                for level in range(1, self.dims + 1):
+                for level in range(self.dims, 0, -1):
                     k = t - level + 1
 
                     @pl.when((k >= 0) & (k < chunks))
                     def _():
                         self.arrivals(k, level, (u - level + 1) % self.dims)
+
+                @pl.when(t + ahead < chunks)
+                def _():
+                    begin(t + ahead, u + ahead)
 
                 work(t - self.dims, (u - self.dims) % 2)
             return carry
@@ -297,7 +301,13 @@
                 errors[k, place, pairs + t * HALF : pairs + (t + 1) * HALF] = odd - w_odd
         cube.pass_on(k, 0, phase)
 
-    nt = min(width, 512)
+    def begin(k, phase):
+        own(k, phase)
+        if isinstance(k, int) and k == 0:
+            for copy in spreads + maps + [keep]:
+                copy.start()
+
+    nt = min(width, 1024)
 
     def multiply(slot, columns):
         part_ref[:, columns] += three_products(e_high[...], e_low[...], h_high[slot][:, columns], h_low[slot][:, columns])
@@ -347,31 +357,28 @@
 
             lax.fori_loop(0, width // nt, alone, 0)
 
-        @pl.when(k == 0)
+        @pl.when(k == -1)
         def _():
             lines_start()
 
         for d in range(1, n_row):
-            @pl.when(k == min(2 * d, chunks - 1))
+            @pl.when(k == (chunks - 1 if d + 1 == n_row else min(2 * d, chunks - 1)))
             def _():
                 lines_pass(d)
-
-    for copy in spreads + maps + [keep]:
-        copy.start()
-    own(0, 0)
-    fetched(0)
 
     def convert_first(n, carry):
         convert(0, rows_of(n, nt))
         return carry
 
-    lax.fori_loop(0, width // nt, convert_first, 0)
-    for copy in out_copies(0, 0):
-        copy.start()
-    if chunks > 2:
-        fetch(2, 0)
-
-    cube.turns(chunks, 0, own, product)
+    def prepare():
+        fetched(0)
+        lax.fori_loop(0, width // nt, convert_first, 0)
+        for copy in out_copies(0, 0):
+            copy.start()
+        if chunks > 2:
+            fetch(2, 0)
+
+    cube.turns(chunks, 0, 2, begin, product, prepare)
     for k in range(max(0, chunks - 2), chunks):
         for copy in out_copies(k, k % 2):
             copy.wait()
@@ -465,7 +472,7 @@
         cube.pass_on(k, 0, phase)
         codes_all[k, rows_of(c, rows), :] = codes_ref[:, rows_of(k, pairs)]
 
-    nt = min(width, 512)
+    nt = min(width, 1024)
     tiles = total_rows // TILE_ROWS
     share = tiles // (width // nt)
 
@@ -526,8 +533,7 @@
             for copy in fetch(k + 1, 1 - slot):
                 copy.start()
 
-    own(0, 0)
-    cube.turns(chunks, 1, own, work)
+    cube.turns(chunks, 1, 3, own, work)
     cube.drain(chunks)
 
 
@@ -555,12 +561,7 @@
     )(maps, codes, delta.reshape(-1, 4, LANES), high, low)
 
 
-def spread_tile(codes, left, right):
-    even, odd = split_pairs(left, right)
-    values = []
-    for x in (even, odd):
-        high = x.astype(jnp.bfloat16).astype(jnp.float32)
-        values += [high, x - high]
+def spread_tile(codes, values):
     upper = codes // LOW
     lower = (codes & (LOW - 1)).astype(jnp.float32).astype(jnp.bfloat16)
     eight = lax.broadcasted_iota(jnp.int32, (8, LANES), 0)
@@ -577,7 +578,7 @@
     )
 
 
-def scatter_kernel(run, gap, sizes, place_ref, map_ref, codes_ref, grad_ref, books_ref, sums_ref):
+def scatter_kernel(run, gap, sizes, place_ref, map_ref, codes_ref, grad_ref, books_ref, sums_ref, planes_ref, order_ref):
     g = pl.program_id(0)
     groups, rows_here, span = codes_ref.shape
     down, across = rows_here // TILE_ROWS, groups * span // HALF
@@ -590,6 +591,18 @@
     @pl.when(g == 0)
     def _():
         sums_ref[...] = jnp.zeros_like(sums_ref)
+        source = lax.broadcasted_iota(jnp.int32, order_ref.shape, 0)
+        target = lax.broadcasted_iota(jnp.int32, order_ref.shape, 1)
+        wanted = jnp.where(target < HALF, 2 * target, 2 * (target - HALF) + 1)
+        order_ref[...] = jnp.where(source == wanted, 1.0, 0.0).astype(jnp.bfloat16)
+
+    def part(j, carry):
+        columns = rows_of(j, TILE_COLS)
+        both = jnp.concatenate(halves(grad_ref[:, columns]), axis=0)
+        planes_ref[:, columns] = jnp.dot(both, order_ref[...], preferred_element_type=jnp.float32)
+        return carry
+
+    lax.fori_loop(0, across, part, 0)
 
     def book(i, column):
         line = top + i
@@ -606,17 +619,17 @@
         i, j = t // across, t % across
         rows = rows_of(i, TILE_ROWS)
         codes = codes_ref[j // (span // HALF), rows, rows_of(j % (span // HALF), HALF)]
-        left = grad_ref[rows, rows_of(2 * j, LANES)]
-        right = grad_ref[rows, rows_of(2 * j + 1, LANES)]
+        low_rows = pl.ds(pl.multiple_of(rows_here + i * TILE_ROWS, TILE_ROWS), TILE_ROWS)
+        values = [planes_ref[at, rows_of(2 * j + odd, HALF)] for odd in range(2) for at in (rows, low_rows)]
         if halves_apart:
-            none = jnp.zeros_like(left)
-            add(book(i, j * TILE_COLS), spread_tile(codes, left, none))
-            add(book(i, j * TILE_COLS + LANES), spread_tile(codes, none, right))
+            left = lax.broadcasted_iota(jnp.int32, codes.shape, 1) < HALF // 2
+            add(book(i, j * TILE_COLS), spread_tile(codes, [jnp.where(left, x, 0.0) for x in values]))
+            add(book(i, j * TILE_COLS + LANES), spread_tile(codes, [jnp.where(left, 0.0, x) for x in values]))
         else:
-            add(book(i, j * TILE_COLS), spread_tile(codes, left, right))
+            add(book(i, j * TILE_COLS), spread_tile(codes, values))
         return carry
 
-    lax.fori_loop(0, down * across, tile, 0, unroll=1 if halves_apart else 4)
+    lax.fori_loop(0, down * across, tile, 0, unroll=1 if halves_apart else 8)
 
     @pl.when(g == pl.num_programs(0) - 1)
     def _():
@@ -650,7 +663,11 @@
         ],
         out_specs=pl.BlockSpec(shape, lambda i: (0, 0)),
         out_shape=jax.ShapeDtypeStruct(shape, jnp.float32),
-        scratch_shapes=[pltpu.VMEM((shape[0] // 4, 16, LANES), jnp.float32)],
+        scratch_shapes=[
+            pltpu.VMEM((shape[0] // 4, 16, LANES), jnp.float32),
+            pltpu.VMEM((2 * block, n), jnp.float32),
+            pltpu.VMEM((TILE_COLS, TILE_COLS), jnp.bfloat16),
+        ],
         compiler_params=pltpu.CompilerParams(vmem_limit_bytes=VMEM_BYTES),
         cost_estimate=pl.CostEstimate(flops=64 * 32 * m * n, bytes_accessed=6 * m * n, transcendentals=0),
         name="scatter",
@@ -661,93 +678,116 @@
     r, c = lax.axis_index("row"), lax.axis_index("col")
     chip, core = c // 2, lax.rem(c, 2)
     chips = n_col // 2
-    half = grad_ref.shape[0] // 2
+    length = grad_ref.shape[0] // PARTS
+    half = length // 2
     wide = half // chips
     thin = wide // n_row
     pair = (r, chip * 2 + 1 - core)
     others = [lax.rem(chip + d, chips) for d in range(chips)]
     lines = [lax.rem(r + d, n_row) for d in range(n_row)]
-
-    barrier = pltpu.get_barrier_semaphore()
-    pl.semaphore_signal(barrier, inc=1, device_id=pair, device_id_type=MESH)
-    for d in range(1, chips):
-        pl.semaphore_signal(barrier, inc=1, device_id=(r, others[d] * 2 + core), device_id_type=MESH)
-    for d in range(1, n_row):
-        pl.semaphore_signal(barrier, inc=1, device_id=(lines[d], c), device_id_type=MESH)
-    pl.semaphore_wait(barrier, chips + n_row - 1)
-
-    pair_send, pair_recv, chip_send, chip_recv, row_send, row_recv, row_send2, row_recv2, chip_send2, chip_recv2, pair_send2, pair_recv2 = sems
-
-    def send(src, dst, sends, recvs, d, device):
+    greet(
+        [pair]
+        + [(r, others[d] * 2 + core) for d in range(1, chips)]
+        + [(lines[d], c) for d in range(1, n_row)]
+    )
+    started = []
+
+    def send(src, dst, stage, q, d, device):
         copy = pltpu.make_async_remote_copy(
-            src_ref=src, dst_ref=dst, send_sem=sends.at[d], recv_sem=recvs.at[d], device_id=device, device_id_type=MESH
+            src_ref=src,
+            dst_ref=dst,
+            send_sem=sems[2 * stage].at[q, d],
+            recv_sem=sems[2 * stage + 1].at[q, d],
+            device_id=device,
+            device_id_type=MESH,
         )
         copy.start()
+        started.append(copy)
         return copy
 
-    def total_of(first, received, copies):
-        for d, copy in enumerate(copies, 1):
+    def part(q, index, size):
+        return pl.ds(pl.multiple_of(q * length + index * size, size), size)
+
+    def received(copies):
+        for copy in copies:
             copy.wait_recv()
-            first = first + received[d]
-        return first
-
-    copies = []
-    swap = send(grad_ref.at[rows_of(1 - core, half)], pair_in, pair_send, pair_recv, 0, pair)
-    swap.wait_recv()
-    pair_sum[...] = grad_ref[rows_of(core, half), :] + pair_in[...]
-    first = [
-        send(pair_sum.at[rows_of(others[d], wide)], chip_in.at[d], chip_send, chip_recv, d, (r, others[d] * 2 + core))
-        for d in range(1, chips)
-    ]
-    chip_sum[...] = total_of(pair_sum[rows_of(chip, wide), :], chip_in, first)
-    second = [
-        send(chip_sum.at[rows_of(lines[d], thin)], row_in.at[d], row_send, row_recv, d, (lines[d], c))
-        for d in range(1, n_row)
-    ]
-    total = total_of(chip_sum[rows_of(r, thin), :], row_in, second)
-    mine = rows_of((core * chips + chip) * n_row + r, thin)
-    change = -learn_rate * (2.0 * total)
-    if final:
-        out_ref[mine, :] = books_ref[mine, :] + (2.0 * delta_ref[mine, :] + change)
-    else:
-        out_ref[mine, :] = change
-    third = [send(out_ref.at[mine], out_ref.at[mine], row_send2, row_recv2, d, (lines[d], c)) for d in range(1, n_row)]
-    for copy in third:
-        copy.wait_recv()
-    piece = rows_of(core * chips + chip, wide)
-    fourth = [
-        send(out_ref.at[piece], out_ref.at[piece], chip_send2, chip_recv2, d, (r, others[d] * 2 + core))
-        for d in range(1, chips)
-    ]
-    for copy in fourth:
-        copy.wait_recv()
-    part = rows_of(core, half)
-    fifth = send(out_ref.at[part], out_ref.at[part], pair_send2, pair_recv2, 0, pair)
-    fifth.wait_recv()
-    for copy in [swap, fifth] + first + second + third + fourth:
+
+    def swap(q, before):
+        return [send(grad_ref.at[part(q, 1 - core, half)], pair_in.at[q], 0, q, 0, pair)]
+
+    def over_chips(q, before):
+        received(before)
+        pair_sum[q] = grad_ref[part(q, core, half), :] + pair_in[q]
+        return [
+            send(pair_sum.at[q, rows_of(others[d], wide)], chip_in.at[q, d], 1, q, d, (r, others[d] * 2 + core))
+            for d in range(1, chips)
+        ]
+
+    def over_rows(q, before):
+        received(before)
+        total = pair_sum[q, rows_of(chip, wide), :]
+        for d in range(1, chips):
+            total = total + chip_in[q, d]
+        chip_sum[q] = total
+        return [
+            send(chip_sum.at[q, rows_of(lines[d], thin)], row_in.at[q, d], 2, q, d, (lines[d], c))
+            for d in range(1, n_row)
+        ]
+
+    def change(q, before):
+        received(before)
+        total = chip_sum[q, rows_of(r, thin), :]
+        for d in range(1, n_row):
+            total = total + row_in[q, d]
+        mine = part(q, (core * chips + chip) * n_row + r, thin)
+        step = -learn_rate * (2.0 * total)
+        if final:
+            step = books_ref[mine, :] + (2.0 * delta_ref[mine, :] + step)
+        out_ref[mine, :] = step
+        return [send(out_ref.at[mine], out_ref.at[mine], 3, q, d, (lines[d], c)) for d in range(1, n_row)]
+
+    def to_chips(q, before):
+        received(before)
+        piece = part(q, core * chips + chip, wide)
+        return [
+            send(out_ref.at[piece], out_ref.at[piece], 4, q, d, (r, others[d] * 2 + core)) for d in range(1, chips)
+        ]
+
+    def to_pair(q, before):
+        received(before)
+        piece = part(q, core, half)
+        return [send(out_ref.at[piece], out_ref.at[piece], 5, q, 0, pair)]
+
+    before = [[] for _ in range(PARTS)]
+    for stage in (swap, over_chips, over_rows, change, to_chips, to_pair):
+        for q in range(PARTS):
+            before[q] = stage(q, before[q])
+    for copies in before:
+        received(copies)
+    for copy in started:
         copy.wait_send()
 
 
 def update(n_row, n_col, final, grad, books, delta):
-    half = grad.shape[0] // 2
+    half = grad.shape[0] // PARTS // 2
     chips = n_col // 2
     wide = half // chips
     thin = wide // n_row
     dma = pltpu.SemaphoreType.DMA
-    sizes = [1, 1, chips, chips, n_row, n_row, n_row, n_row, chips, chips, 1, 1]
+    sizes = [1, chips, n_row, n_row, chips, 1]
     return pl.pallas_call(
         functools.partial(update_kernel, n_row, n_col, final),
         in_specs=[VMEM, VMEM, VMEM],
         out_specs=VMEM,
         out_shape=jax.ShapeDtypeStruct(grad.shape, jnp.float32),
         scratch_shapes=[
-            pltpu.VMEM((half, LANES), jnp.float32),
-            pltpu.VMEM((half, LANES), jnp.float32),
-            pltpu.VMEM((chips, wide, LANES), jnp.float32),
-            pltpu.VMEM((wide, LANES), jnp.float32),
-            pltpu.VMEM((n_row, thin, LANES), jnp.float32),
+            pltpu.VMEM((PARTS, half, LANES), jnp.float32),
+            pltpu.VMEM((PARTS, half, LANES), jnp.float32),
+            pltpu.VMEM((PARTS, chips, wide, LANES), jnp.float32),
+            pltpu.VMEM((PARTS, wide, LANES), jnp.float32),
+            pltpu.VMEM((PARTS, n_row, thin, LANES), jnp.float32),
         ]
-        + [dma((size,)) for size in sizes],
+        + [dma((PARTS, size)) for size in sizes for _ in range(2)],
         compiler_params=pltpu.CompilerParams(collective_id=2 if final else 0, has_side_effects=True),
         name="last_update" if final else "update",
     )(grad, books, delta)

time: 263 us -> 250 us (0.951)
  Pallas kernels: 259 us -> 246 us
    pallas_call x2, Pallas kernels: 62.8 us -> 54.2 us  [update(): pl.pallas_call(functools.partial(update_kernel, n_row, n_col, final), in_...]
    pallas_call x1, Pallas kernels: 79.8 us -> 75.3 us  [first_product(): pl.pallas_call(functools.partial(first_kernel, n_row, n_col, chunks, run)...]
    pallas_call x2, Pallas kernels: 66 us -> 63.3 us  [scatter(): pl.pallas_call(functools.partial(scatter_kernel, run, gap, sizes), grid=(...]
where the time goes in v3:
time: 250 us; the launch traced here: 249 us
  Pallas kernels  246 us (98%)
  local copies, waits for them, and re-layouts  3.83 us (2%)
    pallas_call x1, Pallas kernels, first_product(): pl.pallas_call(functools.partial(first_kernel, n_row, n_col, chunks, run)...  75.3 us
    pallas_call x2, Pallas kernels, scatter(): pl.pallas_call(functools.partial(scatter_kernel, run, gap, sizes), grid=(...  63.3 us
    pallas_call x2, Pallas kernels, update(): pl.pallas_call(functools.partial(update_kernel, n_row, n_col, final), in_...  54.2 us
    pallas_call x1, Pallas kernels, next_product(): pl.pallas_call(functools.partial(next_kernel, n_col, chunks, down), in_sp...  52.8 us

profile of v3, /device:TPU:0, one launch (start us, length us, event | category | flops | bytes accessed | tf_op | source)
XLA Modules:
  0.0 249.4 jit_solution(3308337782129119035)
XLA Ops:
  0.0 1.3 pad.4.padded_ref
  1.3 75.3 %first_product.1 = (f32[512,2048]{1,0:T(8,128)}, bf16[8,512,2048]{2,1,0:T(8,128)(2,1)}, bf16[8,512,2048]{2,1,0:T(8,128)(2,1)}, s32[4,512,256]{2,1,0:T(8,128)}, s32[4,8,8,128]{3,2,1,0:T(8,128)}) custom-call(s32[4,16]{1,0:T(4,128)} %map_ref.1, s32[8,128]{1,0:T(8,128)} %pad.4.padded_ref, s32[64,2048]{1,0:T(8,128)} %codes_ref.3, bf16[64,4096]{1,0:T(8,128)(2,1)} %weights_ref.1, ...), custom_call_target="tpu_custom_call" | custom-call | flops 25769803776 | bytes 67108864 | tf_op jit(solution)/shard_map/first_product/pallas_call | solution.py:401
  76.6 31.6 %scatter.2.grad_ref = f32[2048,128]{1,0:T(8,128)} custom-call(s32[1]{0:T(128)} %bitcast.place_ref, s32[4,8,8,128]{3,2,1,0:T(8,128)} %get-tuple-element.10.map_ref, s32[4,512,256]{2,1,0:T(8,128)} %get-tuple-element.11.codes_ref, f32[512,2048]{1,0:T(8,128)} %get-tuple-element.12.grad_ref), custom_call_target="tpu_custom_call" | custom-call | flops 2147483648 | bytes 6291456 | tf_op jit(solution)/shard_map/scatter/pallas_call | solution.py:655
  108.2 26.9 %update.1.delta_ref = f32[2048,128]{1,0:T(8,128)} custom-call(f32[2048,128]{1,0:T(8,128)} %scatter.2.grad_ref, f32[2048,128]{1,0:T(8,128)} %bitcast.16, f32[2048,128]{1,0:T(8,128)} %bitcast.17), custom_call_target="tpu_custom_call" | custom-call | tf_op jit(solution)/shard_map/update/pallas_call | solution.py:778
  135.2 52.8 %next_product.1.grad_ref = f32[512,2048]{1,0:T(8,128)} custom-call(s32[4,8,8,128]{3,2,1,0:T(8,128)} %get-tuple-element.10.map_ref, s32[64,2048]{1,0:T(8,128)} %codes_ref.3, f32[512,4,128]{2,1,0:T(4,128)} %bitcast.20, bf16[8,512,2048]{2,1,0:T(8,128)(2,1)} %get-tuple-element.13.high_ref, bf16[8,512,2048]{2,1,0:T(8,128)(2,1)} %get-tuple-element.14.low_ref), custom_call_target="tpu_custom_call" | custom-call | flops 25769803776 | bytes 33554432 | tf_op jit(solution)/shard_map/next_product/pallas_call | solution.py:548
  188.0 31.6 %scatter.3.grad_ref = f32[2048,128]{1,0:T(8,128)} custom-call(s32[1]{0:T(128)} %bitcast.place_ref, s32[4,8,8,128]{3,2,1,0:T(8,128)} %get-tuple-element.10.map_ref, s32[4,512,256]{2,1,0:T(8,128)} %get-tuple-element.11.codes_ref, f32[512,2048]{1,0:T(8,128)} %next_product.1.grad_ref), custom_call_target="tpu_custom_call" | custom-call | flops 2147483648 | bytes 6291456 | tf_op jit(solution)/shard_map/scatter/pallas_call | solution.py:655
  219.6 27.3 %last_update.1 = f32[2048,128]{1,0:T(8,128)} custom-call(f32[2048,128]{1,0:T(8,128)} %scatter.3.grad_ref, f32[2048,128]{1,0:T(8,128)} %bitcast.18, f32[2048,128]{1,0:T(8,128)} %update.1.delta_ref), custom_call_target="tpu_custom_call" | custom-call | tf_op jit(solution)/shard_map/last_update/pallas_call | solution.py:778
  246.9 2.6 %copy.9 = f32[512,2,256]{2,1,0:T(2,128)} copy(f32[512,2,256]{2,1,0:T(2,128)} %bitcast.19) | data formatting | bytes 2097152

commit v4 on v3

--- a/solution.py
+++ b/solution.py
@@ -14,7 +14,7 @@
 HALF = TILE_COLS // 2
 CHUNK_TILES = 2
 LOW = 32
-PARTS = 2
+BOOK_LINES = 16
 
 learn_rate = 0.01
 MESH = pl.DeviceIdType.MESH
@@ -533,7 +533,7 @@
             for copy in fetch(k + 1, 1 - slot):
                 copy.start()
 
-    cube.turns(chunks, 1, 3, own, work)
+    cube.turns(chunks, 1, 2, own, work)
     cube.drain(chunks)
 
 
@@ -613,7 +613,7 @@
         even, odd = sums[0:8] + sums[8:16], sums[16:24] + sums[24:32]
         first = jnp.where(row < 4, even, jnp.concatenate([odd[4:8], odd[0:4]], axis=0))
         second = jnp.where(row < 4, jnp.concatenate([even[4:8], even[0:4]], axis=0), odd)
-        sums_ref[index, :, 0:LOW] += jnp.concatenate([first, second], axis=0)
+        sums_ref[rows_of(index, BOOK_LINES), 0:LOW] += jnp.concatenate([first, second], axis=0)
 
     def tile(t, carry):
         i, j = t // across, t % across
@@ -633,20 +633,18 @@
 
     @pl.when(g == pl.num_programs(0) - 1)
     def _():
-        count = sums_ref.shape[0]
         groups = LANES // LOW
-        step = 16
-        size = step * 4
+        size = 64
 
         def squeeze(n, carry):
-            x = sums_ref[rows_of(n, step)].reshape(size, groups, LANES)
-            total = x[:, 0, :]
+            at = pl.multiple_of(n * size * groups, size * groups)
+            total = sums_ref[pl.ds(at, size, stride=groups), :]
             for b in range(1, groups):
-                total = total + pltpu.roll(x[:, b, :], b * LOW, 1)
+                total = total + pltpu.roll(sums_ref[pl.ds(at + b, size, stride=groups), :], b * LOW, 1)
             books_ref[rows_of(n, size), :] = total
             return carry
 
-        lax.fori_loop(0, count // step, squeeze, 0)
+        lax.fori_loop(0, books_ref.shape[0] // size, squeeze, 0)
 
 
 def scatter(run, gap, sizes, begin, maps, codes, grad, shape):
@@ -664,7 +662,7 @@
         out_specs=pl.BlockSpec(shape, lambda i: (0, 0)),
         out_shape=jax.ShapeDtypeStruct(shape, jnp.float32),
         scratch_shapes=[
-            pltpu.VMEM((shape[0] // 4, 16, LANES), jnp.float32),
+            pltpu.VMEM((shape[0] // 4 * BOOK_LINES, LANES), jnp.float32),
             pltpu.VMEM((2 * block, n), jnp.float32),
             pltpu.VMEM((TILE_COLS, TILE_COLS), jnp.bfloat16),
         ],
@@ -674,11 +672,11 @@
     )(begin, maps, codes, grad)
 
 
-def update_kernel(n_row, n_col, final, grad_ref, books_ref, delta_ref, out_ref, pair_in, pair_sum, chip_in, chip_sum, row_in, *sems):
+def update_kernel(n_row, n_col, parts, grad_ref, out_ref, pair_in, pair_sum, chip_in, chip_sum, row_in, *sems):
     r, c = lax.axis_index("row"), lax.axis_index("col")
     chip, core = c // 2, lax.rem(c, 2)
     chips = n_col // 2
-    length = grad_ref.shape[0] // PARTS
+    length = grad_ref.shape[0] // parts
     half = length // 2
     wide = half // chips
     thin = wide // n_row
@@ -740,10 +738,7 @@
         for d in range(1, n_row):
             total = total + row_in[q, d]
         mine = part(q, (core * chips + chip) * n_row + r, thin)
-        step = -learn_rate * (2.0 * total)
-        if final:
-            step = books_ref[mine, :] + (2.0 * delta_ref[mine, :] + step)
-        out_ref[mine, :] = step
+        out_ref[mine, :] = -learn_rate * (2.0 * total)
         return [send(out_ref.at[mine], out_ref.at[mine], 3, q, d, (lines[d], c)) for d in range(1, n_row)]
 
     def to_chips(q, before):
@@ -758,9 +753,9 @@
         piece = part(q, core, half)
         return [send(out_ref.at[piece], out_ref.at[piece], 5, q, 0, pair)]
 
-    before = [[] for _ in range(PARTS)]
+    before = [[] for _ in range(parts)]
     for stage in (swap, over_chips, over_rows, change, to_chips, to_pair):
-        for q in range(PARTS):
+        for q in range(parts):
             before[q] = stage(q, before[q])
     for copies in before:
         received(copies)
@@ -768,29 +763,30 @@
         copy.wait_send()
 
 
-def update(n_row, n_col, final, grad, books, delta):
-    half = grad.shape[0] // PARTS // 2
+def update(n_row, n_col, grad):
     chips = n_col // 2
+    parts = 4 if grad.shape[0] % (4 * 2 * chips * n_row * 8) == 0 else 2
+    half = grad.shape[0] // parts // 2
     wide = half // chips
     thin = wide // n_row
     dma = pltpu.SemaphoreType.DMA
     sizes = [1, chips, n_row, n_row, chips, 1]
     return pl.pallas_call(
-        functools.partial(update_kernel, n_row, n_col, final),
-        in_specs=[VMEM, VMEM, VMEM],
+        functools.partial(update_kernel, n_row, n_col, parts),
+        in_specs=[VMEM],
         out_specs=VMEM,
         out_shape=jax.ShapeDtypeStruct(grad.shape, jnp.float32),
         scratch_shapes=[
-            pltpu.VMEM((PARTS, half, LANES), jnp.float32),
-            pltpu.VMEM((PARTS, half, LANES), jnp.float32),
-            pltpu.VMEM((PARTS, chips, wide, LANES), jnp.float32),
-            pltpu.VMEM((PARTS, wide, LANES), jnp.float32),
-            pltpu.VMEM((PARTS, n_row, thin, LANES), jnp.float32),
+            pltpu.VMEM((parts, half, LANES), jnp.float32),
+            pltpu.VMEM((parts, half, LANES), jnp.float32),
+            pltpu.VMEM((parts, chips, wide, LANES), jnp.float32),
+            pltpu.VMEM((parts, wide, LANES), jnp.float32),
+            pltpu.VMEM((parts, n_row, thin, LANES), jnp.float32),
         ]
-        + [dma((PARTS, size)) for size in sizes for _ in range(2)],
-        compiler_params=pltpu.CompilerParams(collective_id=2 if final else 0, has_side_effects=True),
-        name="last_update" if final else "update",
-    )(grad, books, delta)
+        + [dma((parts, size)) for size in sizes for _ in range(2)],
+        compiler_params=pltpu.CompilerParams(collective_id=0, has_side_effects=True),
+        name="update",
+    )(grad)
 
 
 def per_device(n_row, n_col, hessian, weights, codes, tile_map, codebooks):
@@ -808,9 +804,9 @@
         spread = lax.dynamic_slice(spread, (0, 0, lax.rem(c * (run // 2), span)), (groups, m, run // 2))
         spread = spread.transpose(1, 0, 2).reshape(1, m, groups * (run // 2))
     split = functools.partial(scatter, run, n_col * run, (down, across), begin, maps, spread)
-    delta = update(n_row, n_col, False, split(grad, books.shape), books, books)
+    delta = update(n_row, n_col, split(grad, books.shape))
     grad = next_product(n_col, down, maps, codes, delta, high, low)
-    books = update(n_row, n_col, True, split(grad, books.shape), books, delta)
+    books = books + (2.0 * delta + update(n_row, n_col, split(grad, books.shape)))
     return books.reshape(count, entries // LANES, parts, LANES).transpose(0, 2, 1, 3).reshape(codebooks.shape)
 
 

time: 250 us -> 243 us (0.972)
  Pallas kernels: 246 us -> 239 us
  other arithmetic: 0 us -> 2.65 us
  local copies, waits for them, and re-layouts: 3.83 us -> 1.28 us
    pallas_call x2, Pallas kernels: 63.3 us -> 60.4 us  [scatter(): pl.pallas_call(functools.partial(scatter_kernel, run, gap, sizes), grid=(...]
    add x0 -> x1, other arithmetic: none -> 2.65 us  [per_device(): books + (2.0 * delta + update(n_row, n_col, split(grad, books.shape)))]
    unnamed x1 -> x2, local copies, waits for them, and re-layouts: 2.55 us -> 0.01 us
where the time goes in v4:
time: 243 us
  Pallas kernels  239 us (98%)
  other arithmetic  2.65 us (1%)
    pallas_call x1, Pallas kernels, first_product(): pl.pallas_call(functools.partial(first_kernel, n_row, n_col, chunks, run)...  75.3 us
    pallas_call x2, Pallas kernels, scatter(): pl.pallas_call(functools.partial(scatter_kernel, run, gap, sizes), grid=(...  60.4 us
    pallas_call x2, Pallas kernels, update(): pl.pallas_call(functools.partial(update_kernel, n_row, n_col, parts), in_...  51.9 us
    pallas_call x1, Pallas kernels, next_product(): pl.pallas_call(functools.partial(next_kernel, n_col, chunks, down), in_sp...  51.3 us

profile of v4, /device:TPU:0, one launch (start us, length us, event | category | flops | bytes accessed | tf_op | source)
XLA Modules:
  0.0 242.9 jit_solution(15399165548931297555)
XLA Ops:
  0.0 1.3 pad.4.padded_ref
  1.3 75.3 %first_product.1 = (f32[512,2048]{1,0:T(8,128)}, bf16[8,512,2048]{2,1,0:T(8,128)(2,1)}, bf16[8,512,2048]{2,1,0:T(8,128)(2,1)}, s32[4,512,256]{2,1,0:T(8,128)}, s32[4,8,8,128]{3,2,1,0:T(8,128)}) custom-call(s32[4,16]{1,0:T(4,128)} %map_ref.1, s32[8,128]{1,0:T(8,128)} %pad.4.padded_ref, s32[64,2048]{1,0:T(8,128)} %codes_ref.3, bf16[64,4096]{1,0:T(8,128)(2,1)} %weights_ref.1, ...), custom_call_target="tpu_custom_call" | custom-call | flops 25769803776 | bytes 67108864 | tf_op jit(solution)/shard_map/first_product/pallas_call | solution.py:401
  76.6 30.2 %scatter.2.grad_ref = f32[2048,128]{1,0:T(8,128)} custom-call(s32[1]{0:T(128)} %bitcast.3.place_ref, s32[4,8,8,128]{3,2,1,0:T(8,128)} %get-tuple-element.10.map_ref, s32[4,512,256]{2,1,0:T(8,128)} %get-tuple-element.11.codes_ref, f32[512,2048]{1,0:T(8,128)} %get-tuple-element.12.grad_ref), custom_call_target="tpu_custom_call" | custom-call | flops 2147483648 | bytes 6291456 | tf_op jit(solution)/shard_map/scatter/pallas_call | solution.py:653
  106.8 26.2 %update.2 = f32[2048,128]{1,0:T(8,128)} custom-call(f32[2048,128]{1,0:T(8,128)} %scatter.2.grad_ref), custom_call_target="tpu_custom_call" | custom-call | tf_op jit(solution)/shard_map/update/pallas_call | solution.py:774
  133.0 0.0 copy-start
  133.0 51.3 %next_product.1.grad_ref = f32[512,2048]{1,0:T(8,128)} custom-call(s32[4,8,8,128]{3,2,1,0:T(8,128)} %get-tuple-element.10.map_ref, s32[64,2048]{1,0:T(8,128)} %codes_ref.3, f32[512,4,128]{2,1,0:T(4,128)} %bitcast.15, bf16[8,512,2048]{2,1,0:T(8,128)(2,1)} %get-tuple-element.13.high_ref, bf16[8,512,2048]{2,1,0:T(8,128)(2,1)} %get-tuple-element.14.low_ref), custom_call_target="tpu_custom_call" | custom-call | flops 25769803776 | bytes 33554432 | tf_op jit(solution)/shard_map/next_product/pallas_call | solution.py:548
  184.3 30.2 %scatter.3.grad_ref = f32[2048,128]{1,0:T(8,128)} custom-call(s32[1]{0:T(128)} %bitcast.3.place_ref, s32[4,8,8,128]{3,2,1,0:T(8,128)} %get-tuple-element.10.map_ref, s32[4,512,256]{2,1,0:T(8,128)} %get-tuple-element.11.codes_ref, f32[512,2048]{1,0:T(8,128)} %next_product.1.grad_ref), custom_call_target="tpu_custom_call" | custom-call | flops 2147483648 | bytes 6291456 | tf_op jit(solution)/shard_map/scatter/pallas_call | solution.py:653
  214.5 25.7 %update.3 = f32[2048,128]{1,0:T(8,128)} custom-call(f32[2048,128]{1,0:T(8,128)} %scatter.3.grad_ref), custom_call_target="tpu_custom_call" | custom-call | tf_op jit(solution)/shard_map/update/pallas_call | solution.py:774
  240.2 0.0 copy-done
  240.2 2.7 %add_add_fusion = f32[2048,128]{1,0:T(8,128)} fusion(f32[2048,128]{1,0:T(8,128)} %bitcast.17, f32[2048,128]{1,0:T(8,128)} %update.3, f32[2048,128]{1,0:T(8,128)S(1)} %copy-done), kind=kLoop, calls=%fused_computation | loop fusion | flops 786432 | bytes 4194304 | tf_op jit(solution)/shard_map/add | solution.py:809
Async XLA Ops:
  133.0 107.3 %copy-start = (f32[2048,128]{1,0:T(8,128)S(1)}, f32[2048,128]{1,0:T(8,128)}, u32[]{:S(2)}) copy-start(f32[2048,128]{1,0:T(8,128)} %update.2) | copy-start | bytes 3145732

commit v5 on v4

--- a/solution.py
+++ b/solution.py
@@ -307,7 +307,7 @@
             for copy in spreads + maps + [keep]:
                 copy.start()
 
-    nt = min(width, 1024)
+    nt = min(width, 2048)
 
     def multiply(slot, columns):
         part_ref[:, columns] += three_products(e_high[...], e_low[...], h_high[slot][:, columns], h_low[slot][:, columns])
@@ -472,7 +472,7 @@
         cube.pass_on(k, 0, phase)
         codes_all[k, rows_of(c, rows), :] = codes_ref[:, rows_of(k, pairs)]
 
-    nt = min(width, 1024)
+    nt = min(width, 2048)
     tiles = total_rows // TILE_ROWS
     share = tiles // (width // nt)
 

time: 243 us -> 241 us (level)
  no operation moved by 1% of the time
where the time goes in v5:
time: 241 us
  Pallas kernels  237 us (98%)
  other arithmetic  2.65 us (1%)
    pallas_call x1, Pallas kernels, first_product(): pl.pallas_call(functools.partial(first_kernel, n_row, n_col, chunks, run)...  73.8 us
    pallas_call x2, Pallas kernels, scatter(): pl.pallas_call(functools.partial(scatter_kernel, run, gap, sizes), grid=(...  60.4 us
    pallas_call x1, Pallas kernels, next_product(): pl.pallas_call(functools.partial(next_kernel, n_col, chunks, down), in_sp...  51.5 us
    pallas_call x2, Pallas kernels, update(): pl.pallas_call(functools.partial(update_kernel, n_row, n_col, parts), in_...  51.4 us

profile of v5, /device:TPU:0, one launch (start us, length us, event | category | flops | bytes accessed | tf_op | source)
XLA Modules:
  0.0 241.2 jit_solution(16390611365794421112)
XLA Ops:
  0.0 1.3 pad.4.padded_ref
  1.3 73.8 %first_product.1 = (f32[512,2048]{1,0:T(8,128)}, bf16[8,512,2048]{2,1,0:T(8,128)(2,1)}, bf16[8,512,2048]{2,1,0:T(8,128)(2,1)}, s32[4,512,256]{2,1,0:T(8,128)}, s32[4,8,8,128]{3,2,1,0:T(8,128)}) custom-call(s32[4,16]{1,0:T(4,128)} %map_ref.1, s32[8,128]{1,0:T(8,128)} %pad.4.padded_ref, s32[64,2048]{1,0:T(8,128)} %codes_ref.3, bf16[64,4096]{1,0:T(8,128)(2,1)} %weights_ref.1, ...), custom_call_target="tpu_custom_call" | custom-call | flops 25769803776 | bytes 67108864 | tf_op jit(solution)/shard_map/first_product/pallas_call | solution.py:401
  75.1 30.2 %scatter.2.grad_ref = f32[2048,128]{1,0:T(8,128)} custom-call(s32[1]{0:T(128)} %bitcast.3.place_ref, s32[4,8,8,128]{3,2,1,0:T(8,128)} %get-tuple-element.10.map_ref, s32[4,512,256]{2,1,0:T(8,128)} %get-tuple-element.11.codes_ref, f32[512,2048]{1,0:T(8,128)} %get-tuple-element.12.grad_ref), custom_call_target="tpu_custom_call" | custom-call | flops 2147483648 | bytes 6291456 | tf_op jit(solution)/shard_map/scatter/pallas_call | solution.py:653
  105.3 25.7 %update.2 = f32[2048,128]{1,0:T(8,128)} custom-call(f32[2048,128]{1,0:T(8,128)} %scatter.2.grad_ref), custom_call_target="tpu_custom_call" | custom-call | tf_op jit(solution)/shard_map/update/pallas_call | solution.py:774
  131.0 0.0 copy-start
  131.0 51.5 %next_product.1.grad_ref = f32[512,2048]{1,0:T(8,128)} custom-call(s32[4,8,8,128]{3,2,1,0:T(8,128)} %get-tuple-element.10.map_ref, s32[64,2048]{1,0:T(8,128)} %codes_ref.3, f32[512,4,128]{2,1,0:T(4,128)} %bitcast.15, bf16[8,512,2048]{2,1,0:T(8,128)(2,1)} %get-tuple-element.13.high_ref, bf16[8,512,2048]{2,1,0:T(8,128)(2,1)} %get-tuple-element.14.low_ref), custom_call_target="tpu_custom_call" | custom-call | flops 25769803776 | bytes 33554432 | tf_op jit(solution)/shard_map/next_product/pallas_call | solution.py:548
  182.6 30.2 %scatter.3.grad_ref = f32[2048,128]{1,0:T(8,128)} custom-call(s32[1]{0:T(128)} %bitcast.3.place_ref, s32[4,8,8,128]{3,2,1,0:T(8,128)} %get-tuple-element.10.map_ref, s32[4,512,256]{2,1,0:T(8,128)} %get-tuple-element.11.codes_ref, f32[512,2048]{1,0:T(8,128)} %next_product.1.grad_ref), custom_call_target="tpu_custom_call" | custom-call | flops 2147483648 | bytes 6291456 | tf_op jit(solution)/shard_map/scatter/pallas_call | solution.py:653
  212.8 25.7 %update.3 = f32[2048,128]{1,0:T(8,128)} custom-call(f32[2048,128]{1,0:T(8,128)} %scatter.3.grad_ref), custom_call_target="tpu_custom_call" | custom-call | tf_op jit(solution)/shard_map/update/pallas_call | solution.py:774
  238.5 0.0 copy-done
  238.5 2.7 %add_add_fusion = f32[2048,128]{1,0:T(8,128)} fusion(f32[2048,128]{1,0:T(8,128)} %bitcast.17, f32[2048,128]{1,0:T(8,128)} %update.3, f32[2048,128]{1,0:T(8,128)S(1)} %copy-done), kind=kLoop, calls=%fused_computation | loop fusion | flops 786432 | bytes 4194304 | tf_op jit(solution)/shard_map/add | solution.py:809
Async XLA Ops:
  131.0 107.5 %copy-start = (f32[2048,128]{1,0:T(8,128)S(1)}, f32[2048,128]{1,0:T(8,128)}, u32[]{:S(2)}) copy-start(f32[2048,128]{1,0:T(8,128)} %update.2) | copy-start | bytes 3145732
